TPU v7x, 256 devices: a whole 4x4x8 slice. The times are simulated.
256 devices in a mesh: space: 128 (over y, z, x), mp: 2 (over core).
Axes of the slice: x: 4, y: 4, z: 8, core: 2. Of those that a mesh axis runs over, the one named last changes fastest.
Arguments:
- points: bfloat16 [262144, 512], P('space'), may hold values from -40 to 40
- curve_rank: int32 [262144], P('space'), may hold values from 0 to 262143, as said below
- patch_counts: int32 [128, 4], P('space'), may hold values from 1 to 1024, 2048 in all within a row
- norm_gain_attn: float32 [512], replicated, may hold values from 0.1 to 1.9
- w_qkv: bfloat16 [3, 512, 512], P(None, None, 'mp'), may hold values from -1.5 to 1.5
- w_out: bfloat16 [512, 512], P('mp'), may hold values from -0.75 to 0.75
- norm_gain_mlp: float32 [512], replicated, may hold values from 0.1 to 1.9
- w_fc1: bfloat16 [512, 2048], P(None, 'mp'), may hold values from -0.25 to 0.25
- w_fc2: bfloat16 [2048, 512], P('mp'), may hold values from -0.1875 to 0.1875
Outputs:
- layer_out: bfloat16 [262144, 512], P('space')
Inputs may be any that keep to these rules, and one draw needn't show every extreme that they name: curve_rank is a permutation; the points of shard a take exactly the positions b * 2048 + a * 16 + m for every owner b and every m below 16. `patch_counts`: each row sums to 2048.
All inputs are finite; a program needn't handle non-finite values.
Results may differ from a plain program's by a relative error of at most 0.0075.
Values may be sent and summed in bfloat16 or wider, within the bound.
A program may use at most 128 MiB of HBM per device.

v0:
```python
import math

import jax
import jax.numpy as jnp
from jax import lax
from jax.sharding import PartitionSpec as P

PATCH = 1024
HDIM = 64


epsilon = 1e-06


def layer_norm(inputs, gain_row):
    values = inputs.astype(jnp.float32)
    average = jnp.mean(values, axis=-1, keepdims=True)
    centred = values - average
    second = jnp.mean(centred * centred, axis=-1, keepdims=True)
    return (centred * lax.rsqrt(second + epsilon) * gain_row).astype(jnp.bfloat16)


def tile_layout(counts, tile_width):
    starts = jnp.cumsum(counts) - counts
    offsets = jnp.arange(tile_width, dtype=jnp.int32)
    usable = offsets[None, :] < counts[:, None]
    source = jnp.where(usable, starts[:, None] + offsets[None, :], 0)
    return (starts, source, usable)


def back_index(starts, length, tile_width):
    places = jnp.arange(length, dtype=jnp.int32)
    covered = starts[None, :] <= places[:, None]
    owning = jnp.sum(covered.astype(jnp.int32), axis=1) - 1
    start_of = jnp.max(jnp.where(covered, starts[None, :], 0), axis=1)
    return owning * tile_width + places - start_of


def attend(queries, key_rows, value_rows, counts):
    length, columns = queries.shape
    head_count = columns // HDIM
    score_scale = 1.0 / math.sqrt(HDIM)
    starts, source, usable = tile_layout(counts, PATCH)

    def one_tile(packed):
        picked, allowed = packed
        tile_q = queries[picked].reshape(PATCH, head_count, HDIM)
        tile_k = key_rows[picked].reshape(PATCH, head_count, HDIM)
        tile_v = value_rows[picked].reshape(PATCH, head_count, HDIM)
        scores = (
            jnp.einsum("qhd,khd->hqk", tile_q, tile_k, preferred_element_type=jnp.float32)
            * score_scale
        )
        scores = jnp.where(allowed[None, None, :], scores, -jnp.inf)
        highest = jnp.max(scores, axis=2, keepdims=True)
        raised = jnp.exp(scores - highest)
        weights = (raised / jnp.sum(raised, axis=2, keepdims=True)).astype(jnp.bfloat16)
        context = jnp.einsum("hqk,khd->qhd", weights, tile_v, preferred_element_type=jnp.float32)
        return context.astype(jnp.bfloat16).reshape(PATCH, columns)

    tile_out = lax.map(one_tile, (source, usable))
    places = back_index(starts, length, PATCH)
    return tile_out.reshape(-1, columns)[places]


def project(arrived, w_qkv):
    queries = jnp.dot(arrived, w_qkv[0], preferred_element_type=jnp.float32).astype(jnp.bfloat16)
    key_rows = jnp.dot(arrived, w_qkv[1], preferred_element_type=jnp.float32).astype(jnp.bfloat16)
    value_rows = jnp.dot(arrived, w_qkv[2], preferred_element_type=jnp.float32).astype(jnp.bfloat16)
    return (queries, key_rows, value_rows)


def body(
    points, curve_rank, patch_counts, norm_gain_attn, w_qkv, w_out, norm_gain_mlp, w_fc1, w_fc2
):
    shards = lax.axis_size("space")
    length, features = points.shape
    cell_rows = length // shards
    half_cols = w_qkv.shape[2]
    own_index = lax.axis_index("space")
    owner_id = curve_rank // length
    within = curve_rank % length - own_index * cell_rows
    slot_of = owner_id * cell_rows + within
    senders = jnp.zeros((length,), jnp.int32).at[slot_of].set(jnp.arange(length, dtype=jnp.int32))
    normed = layer_norm(points, norm_gain_attn)
    ordered_send = normed[senders].reshape(shards, cell_rows, features)
    arrived = lax.all_to_all(
        ordered_send, "space", split_axis=0, concat_axis=0, tiled=True
    ).reshape(length, features)
    queries, key_rows, value_rows = project(arrived, w_qkv)
    context = attend(queries, key_rows, value_rows, patch_counts[0])
    chip_size = lax.axis_size("mp")
    half_rows = length // chip_size
    chip_index = lax.axis_index("mp")
    partial_value = jnp.dot(context, w_out, preferred_element_type=jnp.float32)
    summed = lax.psum_scatter(partial_value, "mp", scatter_dimension=1, tiled=True).astype(
        jnp.bfloat16
    )
    returned = lax.all_to_all(
        summed.reshape(shards, cell_rows, half_cols),
        "space",
        split_axis=0,
        concat_axis=0,
        tiled=True,
    )
    returned = returned.reshape(length, half_cols)[slot_of]
    attn_out = lax.all_gather(returned, "mp", axis=1, tiled=True)
    middle = (points.astype(jnp.float32) + attn_out.astype(jnp.float32)).astype(jnp.bfloat16)
    normed_mlp = layer_norm(middle, norm_gain_mlp)
    hidden = jax.nn.gelu(
        jnp.dot(normed_mlp, w_fc1, preferred_element_type=jnp.float32), approximate=True
    ).astype(jnp.bfloat16)
    summed_mlp = lax.psum_scatter(
        jnp.dot(hidden, w_fc2, preferred_element_type=jnp.float32).astype(jnp.bfloat16),
        "mp",
        scatter_dimension=0,
        tiled=True,
    ).astype(jnp.float32)
    middle_rows = lax.dynamic_slice_in_dim(middle, chip_index * half_rows, half_rows, 0)
    finished = (middle_rows.astype(jnp.float32) + summed_mlp).astype(jnp.bfloat16)
    return lax.all_gather(finished, "mp", axis=0, tiled=True)


def solution(mesh):
    placed = (
        P("space", None),
        P("space"),
        P("space", None),
        P(),
        P(None, None, "mp"),
        P("mp", None),
        P(),
        P(None, "mp"),
        P("mp", None),
    )
    return jax.shard_map(
        body, mesh=mesh, in_specs=placed, out_specs=P("space", None), check_vma=False
    )
```

profile of v0, /device:TPU:97, one launch (start us, length us, event | category | flops | bytes accessed | tf_op | source)
XLA Modules:
  0.0 429.4 jit_solution(8900344260000890417)
XLA Ops:
  11.7 8.0 %scatter_custom_fusion = s32[2048]{0:T(1024)S(1)} fusion(s32[2048]{0:T(1024)S(1)} %get-tuple-element.62, s32[2048]{0:T(1024)S(1)} %iota.14, s32[]{:T(128)} %constant.44.clone.1), kind=kCustom, calls=%fused_computation.92 | custom fusion | bytes 8196 | tf_op jit(solution)/shard_map/scatter | solution.py:84
  21.9 9.2 %gather_fusion.3 = bf16[2048,512]{1,0:T(8,128)(2,1)} fusion(bf16[2048,512]{1,0:T(8,128)(2,1)S(1)} %fusion.25, s32[2048]{0:T(1024)S(1)} %fusion.54), kind=kCustom, calls=%fused_computation.3 | custom fusion | bytes 4202496 | tf_op jit(solution)/shard_map/gather | solution.py:86
  31.1 13.7 %all-to-all-start = ((bf16[128,16,512]{2,1,0:T(8,128)(2,1)}), bf16[128,16,512]{2,1,0:T(8,128)(2,1)S(1)}, u32[]{:S(2)}, u32[]{:S(2)}) async-start(bf16[128,16,512]{2,1,0:T(8,128)(2,1)} %bitcast.73), calls=%async_computation | async-start | bytes 4194304 | tf_op jit(solution)/shard_map/all_to_all | solution.py:87
  46.1 48.0 %all-to-all-done = bf16[128,16,512]{2,1,0:T(8,128)(2,1)S(1)} async-done(((bf16[128,16,512]{2,1,0:T(8,128)(2,1)}), bf16[128,16,512]{2,1,0:T(8,128)(2,1)S(1)}, u32[]{:S(2)}, u32[]{:S(2)}) %all-to-all-start) | async-done | bytes 2097184 | tf_op jit(solution)/shard_map/all_to_all | solution.py:87
  100.4 178.8 %while.10 = (s32[]{:T(128)}, bf16[4,1024,256]{2,1,0:T(8,128)(2,1)}, s32[4,1024]{1,0:T(4,128)S(1)}, bf16[2048,256]{1,0:T(8,128)(2,1)}, pred[4,1024]{1,0:T(4,128)(...) while((s32[]{:T(128)}, bf16[4,1024,256]{2,1,0:T(8,128)(2,1)}, ...), condition=%wide.region_7.8_spmd, body=%wide.region_4.7_spmd.sunk | while | flops 1099174912 | bytes 44105308 | solution.py:61
  114.5 10.3 %fusion.89 = (f32[4,1024]{1,0:T(4,128)S(1)}, f32[4,1024,1024]{1,2,0:T(8,128)}) fusion(pred[1024]{0:T(1024)(128)(4,1)S(1)} %dynamic-slice_reduce_fusion.2, bf16[1024,4,64]{0,2,1:T(8,128)(2,1)} %bitcast.69, bf16[1024,4,64]{0,2,1:T(8,128)(2,1)} %bitcast.70), kind=kOutput, calls=%fused_computation.103.clone.1 | convolution fusion | flops 553649152 | bytes 17843200 | tf_op jit(solution)/shard_map/while/body/eval_jaxpr/sub | solution.py:56
  124.8 5.9 %gather_fusion = bf16[1024,256]{1,0:T(8,128)(2,1)} fusion(bf16[2048,256]{1,0:T(8,128)(2,1)} %get-tuple-element.131, s32[1024]{0:T(1024)S(1)} %broadcast_clamp_fusion.4), kind=kCustom, calls=%fused_computation.clone.1 | custom fusion | bytes 1052672 | tf_op jit(solution)/shard_map/while/body/eval_jaxpr/gather | solution.py:49
  132.8 8.4 %fusion.90 = bf16[4,64,1024]{2,1,0:T(8,128)(2,1)} fusion(bf16[1024,4,64]{0,2,1:T(8,128)(2,1)} %bitcast.71, f32[4,1024,1024]{1,2,0:T(8,128)} %get-tuple-element.110, f32[4,1024]{1,0:T(4,128)S(1)} %get-tuple-element.111), kind=kOutput, calls=%fused_computation.17.clone.1 | convolution fusion | flops 545521664 | bytes 17842176 | tf_op jit(solution)/shard_map/while/body/eval_jaxpr/hqk,khd->qhd/dot_general | solution.py:58
  159.2 10.3 %fusion.89 = (f32[4,1024]{1,0:T(4,128)S(1)}, f32[4,1024,1024]{1,2,0:T(8,128)}) fusion(pred[1024]{0:T(1024)(128)(4,1)S(1)} %dynamic-slice_reduce_fusion.2, bf16[1024,4,64]{0,2,1:T(8,128)(2,1)} %bitcast.69, bf16[1024,4,64]{0,2,1:T(8,128)(2,1)} %bitcast.70), kind=kOutput, calls=%fused_computation.103.clone.1 | convolution fusion | flops 553649152 | bytes 17843200 | tf_op jit(solution)/shard_map/while/body/eval_jaxpr/sub | solution.py:56
  169.5 5.9 %gather_fusion = bf16[1024,256]{1,0:T(8,128)(2,1)} fusion(bf16[2048,256]{1,0:T(8,128)(2,1)} %get-tuple-element.131, s32[1024]{0:T(1024)S(1)} %broadcast_clamp_fusion.4), kind=kCustom, calls=%fused_computation.clone.1 | custom fusion | bytes 1052672 | tf_op jit(solution)/shard_map/while/body/eval_jaxpr/gather | solution.py:49
  177.5 8.4 %fusion.90 = bf16[4,64,1024]{2,1,0:T(8,128)(2,1)} fusion(bf16[1024,4,64]{0,2,1:T(8,128)(2,1)} %bitcast.71, f32[4,1024,1024]{1,2,0:T(8,128)} %get-tuple-element.110, f32[4,1024]{1,0:T(4,128)S(1)} %get-tuple-element.111), kind=kOutput, calls=%fused_computation.17.clone.1 | convolution fusion | flops 545521664 | bytes 17842176 | tf_op jit(solution)/shard_map/while/body/eval_jaxpr/hqk,khd->qhd/dot_general | solution.py:58
  203.9 10.3 %fusion.89 = (f32[4,1024]{1,0:T(4,128)S(1)}, f32[4,1024,1024]{1,2,0:T(8,128)}) fusion(pred[1024]{0:T(1024)(128)(4,1)S(1)} %dynamic-slice_reduce_fusion.2, bf16[1024,4,64]{0,2,1:T(8,128)(2,1)} %bitcast.69, bf16[1024,4,64]{0,2,1:T(8,128)(2,1)} %bitcast.70), kind=kOutput, calls=%fused_computation.103.clone.1 | convolution fusion | flops 553649152 | bytes 17843200 | tf_op jit(solution)/shard_map/while/body/eval_jaxpr/sub | solution.py:56
  214.2 5.9 %gather_fusion = bf16[1024,256]{1,0:T(8,128)(2,1)} fusion(bf16[2048,256]{1,0:T(8,128)(2,1)} %get-tuple-element.131, s32[1024]{0:T(1024)S(1)} %broadcast_clamp_fusion.4), kind=kCustom, calls=%fused_computation.clone.1 | custom fusion | bytes 1052672 | tf_op jit(solution)/shard_map/while/body/eval_jaxpr/gather | solution.py:49
  222.2 8.4 %fusion.90 = bf16[4,64,1024]{2,1,0:T(8,128)(2,1)} fusion(bf16[1024,4,64]{0,2,1:T(8,128)(2,1)} %bitcast.71, f32[4,1024,1024]{1,2,0:T(8,128)} %get-tuple-element.110, f32[4,1024]{1,0:T(4,128)S(1)} %get-tuple-element.111), kind=kOutput, calls=%fused_computation.17.clone.1 | convolution fusion | flops 545521664 | bytes 17842176 | tf_op jit(solution)/shard_map/while/body/eval_jaxpr/hqk,khd->qhd/dot_general | solution.py:58
  248.6 10.3 %fusion.89 = (f32[4,1024]{1,0:T(4,128)S(1)}, f32[4,1024,1024]{1,2,0:T(8,128)}) fusion(pred[1024]{0:T(1024)(128)(4,1)S(1)} %dynamic-slice_reduce_fusion.2, bf16[1024,4,64]{0,2,1:T(8,128)(2,1)} %bitcast.69, bf16[1024,4,64]{0,2,1:T(8,128)(2,1)} %bitcast.70), kind=kOutput, calls=%fused_computation.103.clone.1 | convolution fusion | flops 553649152 | bytes 17843200 | tf_op jit(solution)/shard_map/while/body/eval_jaxpr/sub | solution.py:56
  266.9 8.4 %fusion.90 = bf16[4,64,1024]{2,1,0:T(8,128)(2,1)} fusion(bf16[1024,4,64]{0,2,1:T(8,128)(2,1)} %bitcast.71, f32[4,1024,1024]{1,2,0:T(8,128)} %get-tuple-element.110, f32[4,1024]{1,0:T(4,128)S(1)} %get-tuple-element.111), kind=kOutput, calls=%fused_computation.17.clone.1 | convolution fusion | flops 545521664 | bytes 17842176 | tf_op jit(solution)/shard_map/while/body/eval_jaxpr/hqk,khd->qhd/dot_general | solution.py:58
  279.2 8.5 %gather_fusion.4 = bf16[2048,256]{1,0:T(8,128)(2,1)S(1)} fusion(bf16[4096,256]{1,0:T(8,128)(2,1)} %bitcast.68, s32[2048]{0:T(1024)S(1)} %copy-done.5), kind=kCustom, calls=%fused_computation.4 | custom fusion | bytes 2105344 | tf_op jit(solution)/shard_map/gather | solution.py:63
  290.5 16.4 %reduce-scatter.3.cloned.1.call-done = f32[2048,256]{1,0:T(8,128)} async-done(((f32[2048,512]{1,0:T(8,128)}), f32[2048,256]{1,0:T(8,128)}) %reduce-scatter.3.cloned.1.call-update) | async-done | bytes 2097168 | tf_op jit(solution)/shard_map/reduce_scatter | solution.py:96
  308.6 40.9 %all_to_all.10 = bf16[128,16,256]{2,1,0:T(8,128)(2,1)S(1)} all-to-all(bf16[128,16,256]{2,1,0:T(8,128)(2,1)S(1)} %bitcast.74), channel_id=1, replica_groups=mesh['space'=128,'mp'=2] {'space'}, dimensions={0} | all-to-all | bytes 2097152 | tf_op jit(solution)/shard_map/all_to_all | solution.py:99
  349.5 9.1 %gather_fusion.5 = bf16[2048,256]{1,0:T(8,128)(2,1)} fusion(bf16[2048,256]{1,0:T(8,128)(2,1)S(1)} %bitcast.67, s32[2048]{0:T(1024)S(1)} %copy-done.4), kind=kCustom, calls=%fused_computation.5 | custom fusion | bytes 2105344 | tf_op jit(solution)/shard_map/gather | solution.py:106
  358.9 13.1 %all-gather.6.cloned.1.call-done = bf16[2048,512]{1,0:T(8,128)(2,1)} async-done(((bf16[2048,256]{1,0:T(8,128)(2,1)}), bf16[2048,512]{1,0:T(8,128)(2,1)}) %all-gather.6.cloned.1.call-update) | async-done | bytes 2097168 | tf_op jit(solution)/shard_map/all_gather | solution.py:107
  375.9 7.3 %fusion.32 = bf16[2048,512]{1,0:T(8,128)(2,1)} fusion(bf16[1024,512]{1,0:T(8,128)(2,1)S(1)} %copy-done, bf16[512,1024]{1,0:T(8,128)(2,1)} %param.18, bf16[2048,512]{1,0:T(8,128)(2,1)S(1)} %get-tuple-element.60, f32[512]{0:T(512)S(1)} %copy-done.10, f32[2048]{0:T(1024)S(1)} %add_rsqrt_fusion, f32[2048]{0:T(1024)S(1)} %broadcast_multiply_fusion), kind=kOutput, calls=%fused_computation.50 | convolution fusion | flops 4320133120 | bytes 6309888 | tf_op jit(solution)/shard_map/dot_general | solution.py:114
  383.3 16.5 %reduce-scatter.5.cloned.1.call-done = bf16[1024,512]{1,0:T(8,128)(2,1)} async-done(((bf16[2048,512]{1,0:T(8,128)(2,1)}), bf16[1024,512]{1,0:T(8,128)(2,1)}) %reduce-scatter.5.cloned.1.call-update) | async-done | bytes 1048592 | tf_op jit(solution)/shard_map/reduce_scatter | solution.py:113
  402.3 17.5 %all-gather.4.cloned.1.call-done = bf16[2048,512]{1,0:T(8,128)(2,1)} async-done(((bf16[1024,512]{1,0:T(8,128)(2,1)}), bf16[2048,512]{1,0:T(8,128)(2,1)}) %all-gather.4.cloned.1.call-update) | async-done | bytes 2097168 | tf_op jit(solution)/shard_map/all_gather | solution.py:121
  (100 shorter events, 115.2 us)
Async XLA Ops:
  6.5 369.4 %copy-start = (bf16[1024,512]{1,0:T(8,128)(2,1)S(1)}, bf16[1024,512]{1,0:T(8,128)(2,1)}, u32[]{:S(2)}) copy-start(bf16[1024,512]{1,0:T(8,128)(2,1)} %param.19) | copy-start | bytes 3145732
  6.5 4.5 %copy-start.6 = (s32[2048]{0:T(1024)S(1)}, s32[2048]{0:T(1024)}, u32[]{:S(2)}) copy-start(s32[2048]{0:T(1024)} %param.12) | copy-start | bytes 24580
  6.5 13.2 %copy-start.7 = (f32[512]{0:T(512)S(1)}, f32[512]{0:T(512)}, u32[]{:S(2)}) copy-start(f32[512]{0:T(512)} %param.14) | copy-start | bytes 6148
  31.1 13.9 %copy-start.8 = (s32[1,4]{1,0:T(1,128)S(1)}, s32[1,4]{1,0:T(1,128)}, u32[]{:S(2)}) copy-start(s32[1,4]{1,0:T(1,128)} %param.13) | copy-start | bytes 52
  31.1 63.0 %all-to-all-start = ((bf16[128,16,512]{2,1,0:T(8,128)(2,1)}), bf16[128,16,512]{2,1,0:T(8,128)(2,1)S(1)}, u32[]{:S(2)}, u32[]{:S(2)}) async-start(bf16[128,16,512]{2,1,0:T(8,128)(2,1)} %bitcast.73), calls=%async_computation | async-start | bytes 4194304 | tf_op jit(solution)/shard_map/all_to_all | solution.py:87
  44.7 262.1 %reduce-scatter.3.cloned.1.call-start = ((), (), s32[]{:S(2)}) async-start(), calls=%async_computation.4 | async-start | bytes 6291456 | tf_op jit(solution)/shard_map/reduce_scatter | solution.py:96
  94.1 1.4 copy-start.1
  95.4 2.5 copy-start.9
  95.4 2.6 copy-start.2
  100.4 178.8 %copy-start.5 = (s32[2048]{0:T(1024)S(1)}, s32[2048]{0:T(1024)}, u32[]{:S(2)}) copy-start(s32[2048]{0:T(1024)} %broadcast_clamp_fusion.1) | copy-start | bytes 24580
  279.2 8.6 %copy-start.3 = (bf16[256,512]{1,0:T(8,128)(2,1)S(1)}, bf16[256,512]{1,0:T(8,128)(2,1)}, u32[]{:S(2)}) copy-start(bf16[256,512]{1,0:T(8,128)(2,1)} %param.16) | copy-start | bytes 786436
  290.4 59.1 %copy-start.4 = (s32[2048]{0:T(1024)S(1)}, s32[2048]{0:T(1024)}, u32[]{:S(2)}) copy-start(s32[2048]{0:T(1024)} %get-tuple-element.61) | copy-start | bytes 24580
  290.4 81.5 %all-gather.6.cloned.1.call-start = ((), (), s32[]{:S(2)}) async-start(), calls=%async_computation.7 | async-start | bytes 3145728 | tf_op jit(solution)/shard_map/all_gather | solution.py:107
  358.6 17.4 %copy-start.10 = (f32[512]{0:T(512)S(1)}, f32[512]{0:T(512)}, u32[]{:S(2)}) copy-start(f32[512]{0:T(512)} %param.17) | copy-start | bytes 6148
  358.6 41.2 %reduce-scatter.5.cloned.1.call-start = ((), (), s32[]{:S(2)}) async-start(), calls=%async_computation.5 | async-start | bytes 3145728 | tf_op jit(solution)/shard_map/reduce_scatter | solution.py:113
  383.2 36.5 %all-gather.4.cloned.1.call-start = ((), (), s32[]{:S(2)}) async-start(), calls=%async_computation.6 | async-start | bytes 3145728 | tf_op jit(solution)/shard_map/all_gather | solution.py:121
Sparse Core Ops, SparseCore 0:
  290.6 16.2 reduce-scatter.2
  358.7 13.2 all-gather.5
  383.4 16.3 reduce-scatter.4
  402.4 17.3 all-gather.3
where the time goes:
time: 433 us; the launch traced here: 429 us
  local copies, waits for them, and re-layouts  143 us (33%)
  waiting for transfers between devices  112 us (26%)
  matrix products  89.6 us (21%)
  blocking collectives  40.9 us (9%)
  other arithmetic  16.5 us (4%)
  starting transfers between devices  14.2 us (3%)
  between operations  13.3 us (3%)
    all_to_all x1, waiting for transfers between devices, body(): lax.all_to_all(ordered_send, 'space', split_axis=0, concat_axis=0, tiled=...  48 us
    sub x4, matrix products, one_tile(): raised = jnp.exp(scores - highest)  41.4 us
    all_to_all x1, blocking collectives, body(): lax.all_to_all(summed.reshape(shards, cell_rows, half_cols), 'space', spl...  40.9 us
    dot_general x4, matrix products, one_tile(): jnp.einsum('hqk,khd->qhd', weights, tile_v, preferred_element_type=jnp.fl...  33.5 us
    gather x8, local copies, waits for them, and re-layouts, one_tile(): tile_v = value_rows[picked].reshape(PATCH, head_count, HDIM)  32 us
    gather x8, local copies, waits for them, and re-layouts, one_tile(): tile_q = queries[picked].reshape(PATCH, head_count, HDIM)  28.1 us
    gather x8, local copies, waits for them, and re-layouts, one_tile(): tile_k = key_rows[picked].reshape(PATCH, head_count, HDIM)  28 us
    all_gather x1, waiting for transfers between devices, body(): return lax.all_gather(finished, 'mp', axis=0, tiled=True)  17.5 us
  transfers between devices with their start and end apart: 5, of which 5 were waited for; matrix products, arithmetic and copies ran while one was open for 0% of the time, Pallas kernels for 0%

commit v1 on v0

v1 whole, which is shorter than its diff:
```python
import functools
import math

import jax
import jax.numpy as jnp
from jax import lax
from jax.experimental import pallas as pl
from jax.experimental.pallas import tpu as pltpu
from jax.sharding import PartitionSpec as P

HDIM = 64
EPS = 1e-06
FAR = -1e30
QSCALE = math.log2(math.e) / math.sqrt(HDIM)

LENGTH = 2048
FEAT = 512
HALF = 1024
SHARDS = 128
PEERS = 64
CELL = 16
GROUP = 256
GROUPS = 4
NX, NZ = 4, 8

MESH = pl.DeviceIdType.MESH
VMEM = pltpu.VMEM
F32 = jnp.float32
BF16 = jnp.bfloat16


def dot(a, b):
    return jnp.dot(a, b, preferred_element_type=F32)


def norm_rows(values, gain):
    average = jnp.mean(values, axis=-1, keepdims=True)
    centred = values - average
    second = jnp.mean(centred * centred, axis=-1, keepdims=True)
    return (centred * lax.rsqrt(second + EPS) * gain).astype(BF16)


class Place:
    def __init__(self):
        self.s = lax.axis_index("space")
        self.c = lax.axis_index("mp")
        self.x = lax.rem(self.s, NX)
        self.z = lax.rem(self.s // NX, NZ)
        self.h = self.s // PEERS
        self.own = self.s - self.h * PEERS
        self.partner = (self.s, 1 - self.c)
        self.has_self = self.h == self.c

    def group(self, j):
        near = self.z // (NZ // 2)
        zh = (1 - near) if j < 2 else near
        return (j % 2) * 2 + zh

    def peer(self, group, q):
        zz = lax.rem(q // NX + self.z, NZ // 2)
        xx = lax.rem(q + self.x, NX)
        return group * 16 + zz * NX + xx


def greet(me):
    barrier = pltpu.get_barrier_semaphore()

    def one(i, carry):
        peer = lax.rem(me.own + i, PEERS)

        @pl.when(jnp.logical_not(me.has_self & (i == 0)))
        def _():
            pl.semaphore_signal(
                barrier, inc=1, device_id=(me.c * PEERS + peer, me.h), device_id_type=MESH
            )

        return carry

    lax.fori_loop(0, PEERS, one, 0)
    pl.semaphore_signal(barrier, inc=1, device_id=me.partner, device_id_type=MESH)
    return barrier


def await_greetings(me, barrier):
    pl.semaphore_wait(barrier, jnp.where(me.has_self, PEERS, PEERS + 1))


def send_group(me, group, src, dst, send_sem, recv_sem):
    landing = pl.multiple_of(me.s * CELL, CELL)
    mine = me.own // 16

    def one(q, carry):
        peer = me.peer(group, q)
        rows = pl.ds(pl.multiple_of(peer * CELL, CELL), CELL)
        itself = me.has_self & (peer == me.own)

        @pl.when(itself)
        def _():
            pltpu.make_async_copy(
                src.at[rows], dst.at[pl.ds(landing, CELL)], recv_sem.at[mine]
            ).start()

        @pl.when(jnp.logical_not(itself))
        def _():
            pltpu.make_async_remote_copy(
                src_ref=src.at[rows],
                dst_ref=dst.at[pl.ds(landing, CELL)],
                send_sem=send_sem,
                recv_sem=recv_sem.at[mine],
                device_id=(me.c * PEERS + peer, me.h),
                device_id_type=MESH,
            ).start()

        return carry

    lax.fori_loop(0, 16, one, 0)


def await_sends(me, src, dst, send_sem, recv_sem):
    def over(rows):
        pltpu.make_async_remote_copy(
            src_ref=src.at[pl.ds(0, rows)],
            dst_ref=dst.at[pl.ds(0, rows)],
            send_sem=send_sem,
            recv_sem=recv_sem.at[0],
            device_id=me.partner,
            device_id_type=MESH,
        ).wait_send()

    @pl.when(me.has_self)
    def _():
        over(HALF - CELL)

    @pl.when(jnp.logical_not(me.has_self))
    def _():
        over(HALF)


def relay(me, buf, start, rows, send_sem, recv_sem):
    part = buf.at[pl.ds(start, rows)]
    return pltpu.make_async_remote_copy(
        src_ref=part,
        dst_ref=part,
        send_sem=send_sem,
        recv_sem=recv_sem,
        device_id=me.partner,
        device_id_type=MESH,
    )


def local_slots(rank, s):
    return (rank // LENGTH) * CELL + (rank % LENGTH) - s * CELL


def gather_kernel(
    points, rank, gain, w_qkv, w_out, w_fc1, w_fc2,
    q_ref, k_ref, v_ref, raw_ref, w_out_p, w_fc1_p, w_fc2_p,
    acc, send, arrived, send_sem, recv_sem, rsend_sem, rrecv_sem, wsend_sem, wrecv_sem,
):
    me = Place()
    barrier = greet(me)
    slots = local_slots(rank[...], me.s)

    def permute(group):
        first = me.c * HALF + group * GROUP
        total = jnp.zeros((GROUP, FEAT), F32)
        for part in range(4):
            cols = pl.ds(part * 512, 512)
            wanted = first + lax.broadcasted_iota(jnp.int32, (GROUP, 512), 0)
            hit = wanted == slots[:, part * 512 : (part + 1) * 512]
            pick = jnp.where(hit, 1.0, 0.0).astype(BF16)
            total = total + dot(pick, points[cols, :])
        send[pl.ds(pl.multiple_of(group * GROUP, GROUP), GROUP), :] = total.astype(BF16)

    weights = []
    for i, (src, dst) in enumerate(((w_out, w_out_p), (w_fc1, w_fc1_p), (w_fc2, w_fc2_p))):
        weights.append(
            pltpu.make_async_remote_copy(
                src_ref=src,
                dst_ref=dst,
                send_sem=wsend_sem.at[i],
                recv_sem=wrecv_sem.at[i],
                device_id=me.partner,
                device_id_type=MESH,
            )
        )

    for j in range(GROUPS):
        group = me.group(j)
        permute(group)
        if j == 0:
            await_greetings(me, barrier)
        send_group(me, group, send, arrived, send_sem, recv_sem)
    for copy in weights:
        copy.start()

    def project(start):
        rows = pl.ds(start, GROUP)
        normed = norm_rows(arrived[rows, :].astype(F32), gain[...])
        q_ref[rows, :] = (dot(normed, w_qkv[0]) * QSCALE).astype(BF16)
        k_ref[rows, :] = dot(normed, w_qkv[1]).astype(BF16)
        v_ref[rows, :] = dot(normed, w_qkv[2]).astype(BF16)

    def start_of(half, group):
        return pl.multiple_of(half * HALF + group * GROUP, GROUP)

    for j in range(GROUPS):
        group = me.group(j)
        start = start_of(me.c, group)
        copy = relay(me, arrived, start, GROUP, rsend_sem.at[group], recv_sem.at[group])
        copy.wait_recv()
        relay(me, arrived, start, GROUP, rsend_sem.at[group], rrecv_sem.at[group]).start()
        project(start)
    for j in range(GROUPS):
        group = me.group(j)
        start = start_of(1 - me.c, group)
        relay(me, arrived, start, GROUP, rsend_sem.at[group], rrecv_sem.at[group]).wait_recv()
        project(start)
    raw_ref[...] = arrived[pl.ds(pl.multiple_of(me.c * HALF, HALF), HALF), :]
    for j in range(GROUPS):
        group = me.group(j)
        start = start_of(me.c, group)
        relay(me, arrived, start, GROUP, rsend_sem.at[group], rrecv_sem.at[group]).wait_send()
    await_sends(me, send, arrived, send_sem, recv_sem)
    for copy in weights:
        copy.wait()


def attend_kernel(counts, q, k, v, out, qh, kh, vh, scores, highest, total):
    s1 = counts[0, 0]
    s2 = s1 + counts[0, 1]
    s3 = s2 + counts[0, 2]

    def prepare(i, carry):
        rows = pl.ds(pl.multiple_of(i * 256, 256), 256)
        position = i * 256 + lax.broadcasted_iota(jnp.int32, (256, 128), 0)
        lane = lax.broadcasted_iota(jnp.int32, (256, 128), 1)
        patch = (
            (position >= s1).astype(jnp.int32)
            + (position >= s2).astype(jnp.int32)
            + (position >= s3).astype(jnp.int32)
        )
        mark = lane & (HDIM - 1)
        q_mark = jnp.where(mark == patch, 1.0, 0.0).astype(BF16)
        k_mark = jnp.where((mark < 4) & (mark != patch), FAR, 0.0).astype(BF16)
        ones = jnp.ones((256, 128), BF16)
        for head in range(4):
            pair = slice((head // 2) * 128, (head // 2 + 1) * 128)
            own = (lane // HDIM) == (head % 2)
            qh[head, rows, :] = jnp.where(own, q[rows, pair], q_mark)
            kh[head, rows, :] = jnp.where(own, k[rows, pair], k_mark)
            vh[head, rows, :] = jnp.where(own, v[rows, pair], ones)
        return carry

    lax.fori_loop(0, LENGTH // 256, prepare, 0)

    def block(i, carry):
        q0 = i * 256
        last = q0 + 255
        low = jnp.where(q0 >= s3, s3, jnp.where(q0 >= s2, s2, jnp.where(q0 >= s1, s1, 0)))
        high = jnp.where(
            last < s1, s1, jnp.where(last < s2, s2, jnp.where(last < s3, s3, LENGTH))
        )
        first, end = low // 256, (high + 255) // 256
        rows = pl.ds(pl.multiple_of(q0, 256), 256)
        for head in range(4):
            highest[head] = jnp.full((256, 128), -3e38, F32)
            total[head] = jnp.zeros((256, 128), F32)

        def score(j, carry):
            keys = pl.ds(pl.multiple_of(j * 256, 256), 256)
            for head in range(4):
                value = lax.dot_general(
                    qh[head, rows, :],
                    kh[head, keys, :],
                    (((1,), (1,)), ((), ())),
                    preferred_element_type=F32,
                )
                scores[head, j] = value
                highest[head] = jnp.maximum(
                    highest[head], jnp.maximum(value[:, :128], value[:, 128:])
                )
            return carry

        lax.fori_loop(first, end, score, 0)
        for head in range(4):
            highest[head] = jnp.broadcast_to(
                jnp.max(highest[head], axis=-1, keepdims=True), (256, 128)
            )

        def weigh(j, carry):
            keys = pl.ds(pl.multiple_of(j * 256, 256), 256)
            for head in range(4):
                top = highest[head]
                value = scores[head, j]
                raised = jnp.concatenate(
                    [jnp.exp2(value[:, :128] - top), jnp.exp2(value[:, 128:] - top)], axis=1
                ).astype(BF16)
                total[head] += dot(raised, vh[head, keys, :])
            return carry

        lax.fori_loop(first, end, weigh, 0)
        lane = lax.broadcasted_iota(jnp.int32, (256, 128), 1)
        for pair in range(2):
            done = []
            for head in (2 * pair, 2 * pair + 1):
                value = total[head]
                done.append(value / pltpu.roll(value, HDIM, 1))
            out[rows, pair * 128 : (pair + 1) * 128] = jnp.where(
                lane < HDIM, done[0], done[1]
            ).astype(BF16)
        return carry

    lax.fori_loop(0, LENGTH // 256, block, 0)


def return_kernel(
    ctx, raw, gain, w_out, w_fc1, w_fc2, w_out_p, w_fc1_p, w_fc2_p,
    back_ref, ctx_p, send, send_sem, recv_sem, rsend_sem, rrecv_sem, csend_sem, crecv_sem,
):
    me = Place()
    barrier = greet(me)
    await_greetings(me, barrier)
    own_half = pl.multiple_of(me.c * HALF, HALF)
    other_half = pl.multiple_of((1 - me.c) * HALF, HALF)
    swap = pltpu.make_async_remote_copy(
        src_ref=ctx.at[pl.ds(other_half, HALF)],
        dst_ref=ctx_p,
        send_sem=csend_sem,
        recv_sem=crecv_sem,
        device_id=me.partner,
        device_id_type=MESH,
    )
    swap.start()
    swap.wait_recv()

    def finish(group):
        start = pl.multiple_of(group * GROUP, GROUP)
        rows = pl.ds(start, GROUP)
        own_rows = pl.ds(pl.multiple_of(own_half + start, GROUP), GROUP)
        attn = dot(ctx[own_rows, :], w_out[...]) + dot(ctx_p[rows, :], w_out_p[...])
        middle = (raw[rows, :].astype(F32) + attn.astype(BF16).astype(F32)).astype(BF16).astype(F32)
        normed = norm_rows(middle, gain[...])
        result = middle
        for fc1, fc2 in ((w_fc1, w_fc2), (w_fc1_p, w_fc2_p)):
            hidden = jax.nn.gelu(dot(normed, fc1[...]), approximate=True).astype(BF16)
            result = result + dot(hidden, fc2[...])
        send[rows, :] = result.astype(BF16)

    for j in range(GROUPS):
        group = me.group(j)
        finish(group)
        send_group(me, group, send, back_ref, send_sem, recv_sem)

    def start_of(half, group):
        return pl.multiple_of(half * HALF + group * GROUP, GROUP)

    for j in range(GROUPS):
        group = me.group(j)
        start = start_of(me.c, group)
        relay(me, back_ref, start, GROUP, rsend_sem.at[group], recv_sem.at[group]).wait_recv()
        relay(me, back_ref, start, GROUP, rsend_sem.at[group], rrecv_sem.at[group]).start()
    for j in range(GROUPS):
        group = me.group(j)
        start = start_of(1 - me.c, group)
        relay(me, back_ref, start, GROUP, rsend_sem.at[group], rrecv_sem.at[group]).wait_recv()
    for j in range(GROUPS):
        group = me.group(j)
        start = start_of(me.c, group)
        relay(me, back_ref, start, GROUP, rsend_sem.at[group], rrecv_sem.at[group]).wait_send()
    swap.wait_send()
    await_sends(me, send, back_ref, send_sem, recv_sem)


def place_kernel(rank, back, out):
    s = lax.axis_index("space")
    i = pl.program_id(0)
    slots = local_slots(rank[...], s)
    total = jnp.zeros((256, FEAT), F32)
    columns = [
        jnp.broadcast_to(slots[:, p * 128 : (p + 1) * 128], (128, 128)).T for p in range(2)
    ]
    column = jnp.concatenate(columns, axis=0)
    lane = lax.broadcasted_iota(jnp.int32, (256, 128), 1)
    for part in range(4):
        picks = [
            jnp.where(column == lane + (part * 512 + t * 128), 1.0, 0.0).astype(BF16)
            for t in range(4)
        ]
        total = total + dot(jnp.concatenate(picks, axis=1), back[pl.ds(part * 512, 512), :])
    out[...] = total.astype(BF16)


def body(
    points, curve_rank, patch_counts, norm_gain_attn, w_qkv, w_out, norm_gain_mlp, w_fc1, w_fc2
):
    rank = curve_rank.reshape(1, LENGTH)
    shape = jax.ShapeDtypeStruct
    vm = pl.BlockSpec(memory_space=pltpu.VMEM)
    anywhere = pl.BlockSpec(memory_space=pl.ANY)
    dma = pltpu.SemaphoreType.DMA
    cols = w_qkv.shape[2]
    q, k, v, raw, w_out_p, w_fc1_p, w_fc2_p = pl.pallas_call(
        gather_kernel,
        name="gather_rows",
        out_shape=(
            shape((LENGTH, cols), BF16),
            shape((LENGTH, cols), BF16),
            shape((LENGTH, cols), BF16),
            shape((HALF, FEAT), BF16),
            shape(w_out.shape, BF16),
            shape(w_fc1.shape, BF16),
            shape(w_fc2.shape, BF16),
        ),
        in_specs=[vm] * 4 + [anywhere] * 3,
        out_specs=[vm] * 4 + [anywhere] * 3,
        scratch_shapes=[
            VMEM((GROUP, FEAT), F32),
            VMEM((HALF, FEAT), BF16),
            VMEM((LENGTH, FEAT), BF16),
            dma, dma((4,)), dma((4,)), dma((4,)), dma((3,)), dma((3,)),
        ],
        compiler_params=pltpu.CompilerParams(collective_id=0, has_side_effects=True),
    )(points, rank, norm_gain_attn.reshape(1, FEAT), w_qkv, w_out, w_fc1, w_fc2)

    context = pl.pallas_call(
        attend_kernel,
        name="attend",
        out_shape=shape((LENGTH, cols), BF16),
        in_specs=[pl.BlockSpec(memory_space=pltpu.SMEM)] + [vm] * 3,
        out_specs=vm,
        scratch_shapes=[
            VMEM((4, LENGTH, 128), BF16),
            VMEM((4, LENGTH, 128), BF16),
            VMEM((4, LENGTH, 128), BF16),
            VMEM((4, 8, 256, 256), F32),
            VMEM((4, 256, 128), F32),
            VMEM((4, 256, 128), F32),
        ],
    )(patch_counts, q, k, v)

    back = pl.pallas_call(
        return_kernel,
        name="return_rows",
        out_shape=shape((LENGTH, FEAT), BF16),
        in_specs=[vm] * 9,
        out_specs=vm,
        scratch_shapes=[
            VMEM((HALF, cols), BF16),
            VMEM((HALF, FEAT), BF16),
            dma, dma((4,)), dma((4,)), dma((4,)), dma, dma,
        ],
        compiler_params=pltpu.CompilerParams(collective_id=1, has_side_effects=True),
    )(context, raw, norm_gain_mlp.reshape(1, FEAT), w_out, w_fc1, w_fc2, w_out_p, w_fc1_p, w_fc2_p)

    return pl.pallas_call(
        place_kernel,
        name="place_rows",
        grid=(LENGTH // 256,),
        out_shape=shape((LENGTH, FEAT), BF16),
        in_specs=[
            pl.BlockSpec((1, 256), lambda i: (0, i)),
            pl.BlockSpec((LENGTH, FEAT), lambda i: (0, 0)),
        ],
        out_specs=pl.BlockSpec((256, FEAT), lambda i: (i, 0)),
    )(rank, back)


def solution(mesh):
    placed = (
        P("space", None),
        P("space"),
        P("space", None),
        P(),
        P(None, None, "mp"),
        P("mp", None),
        P(),
        P(None, "mp"),
        P("mp", None),
    )
    return jax.shard_map(
        body, mesh=mesh, in_specs=placed, out_specs=P("space", None), check_vma=False
    )
```

time: 433 us -> 129 us (0.30)
  the two profiles are of different devices: /device:TPU:97 before, /device:TPU:73 now
where the time goes in v1:
time: 129 us
  Pallas kernels  129 us (100%)
    pallas_call x1, Pallas kernels, body(): pl.pallas_call(return_kernel, name='return_rows', out_shape=shape((LENGTH...  46 us
    pallas_call x1, Pallas kernels, body(): pl.pallas_call(gather_kernel, name='gather_rows', out_shape=(shape((LENGT...  44.3 us
    pallas_call x1, Pallas kernels, body(): pl.pallas_call(attend_kernel, name='attend', out_shape=shape((LENGTH, col...  30.2 us
    pallas_call x1, Pallas kernels, body(): pl.pallas_call(place_kernel, name='place_rows', grid=(LENGTH // 256,), ou...  8.49 us

profile of v1, /device:TPU:73, one launch (start us, length us, event | category | flops | bytes accessed | tf_op | source)
XLA Modules:
  0.0 129.1 jit_solution(7777764835242330096)
XLA Ops:
  0.0 44.3 %gather_rows.1 = (bf16[2048,256]{1,0:T(8,128)(2,1)}, bf16[2048,256]{1,0:T(8,128)(2,1)}, bf16[2048,256]{1,0:T(8,128)(2,1)}, bf16[1024,512]{1,0:T(8,128)(2,1)}, bf...) custom-call(bf16[2048,512]{1,0:T(8,128)(2,1)} %points.1, s32[1,2048]{1,0:T(1,128)} %bitcast.3, ...), custom_call_target="tpu_custom_call" | custom-call | tf_op jit(solution)/shard_map/gather_rows/pallas_call | solution.py:403
  44.3 30.2 %attend.1.ctx = bf16[2048,256]{1,0:T(8,128)(2,1)} custom-call(s32[1,4]{1,0:T(1,128)} %counts.1, bf16[2048,256]{1,0:T(8,128)(2,1)} %get-tuple-element.12.q, bf16[2048,256]{1,0:T(8,128)(2,1)} %get-tuple-element.13.k, bf16[2048,256]{1,0:T(8,128)(2,1)} %get-tuple-element.14.v), custom_call_target="tpu_custom_call" | custom-call | tf_op jit(solution)/shard_map/attend/pallas_call | solution.py:426
  74.5 46.0 %return_rows.1.back = bf16[2048,512]{1,0:T(8,128)(2,1)} custom-call(bf16[2048,256]{1,0:T(8,128)(2,1)} %attend.1.ctx, bf16[1024,512]{1,0:T(8,128)(2,1)} %get-tuple-element.15.raw, f32[1,512]{1,0:T(1,128)} %bitcast.6, bf16[256,512]{1,0:T(8,128)(2,1)} %w_out.3, bf16[512,1024]{1,0:T(8,128)(2,1)} %w_fc1.3, bf16[1024,512]{1,0:T(8,128)(2,1)} %w_fc2.3, ...), custom_call_target="tpu_custom_call" | custom-call | tf_op jit(solution)/shard_map/return_rows/pallas_call | solution.py:442
  120.6 8.5 %place_rows.1 = bf16[2048,512]{1,0:T(8,128)(2,1)} custom-call(s32[1,2048]{1,0:T(1,128)} %bitcast.4, bf16[2048,512]{1,0:T(8,128)(2,1)} %return_rows.1.back), custom_call_target="tpu_custom_call" | custom-call | tf_op jit(solution)/shard_map/place_rows/pallas_call | solution.py:456

commit v2 on v1

v2 whole, which is shorter than its diff:
```python
import functools
import math

import jax
import jax.numpy as jnp
from jax import lax
from jax.experimental import pallas as pl
from jax.experimental.pallas import tpu as pltpu
from jax.sharding import PartitionSpec as P

HDIM = 64
EPS = 1e-06
FAR = -1e30
QSCALE = math.log2(math.e) / math.sqrt(HDIM)

LENGTH = 2048
FEAT = 512
HALF = 1024
SHARDS = 128
PEERS = 64
CELL = 16
GROUP = 256
GROUPS = 4
NX, NZ = 4, 8

MESH = pl.DeviceIdType.MESH
VMEM = pltpu.VMEM
F32 = jnp.float32
BF16 = jnp.bfloat16


def dot(a, b):
    return jnp.dot(a, b, preferred_element_type=F32)


def norm_rows(values, gain):
    average = jnp.mean(values, axis=-1, keepdims=True)
    centred = values - average
    second = jnp.mean(centred * centred, axis=-1, keepdims=True)
    return (centred * lax.rsqrt(second + EPS) * gain).astype(BF16)


class Place:
    def __init__(self):
        self.s = lax.axis_index("space")
        self.c = lax.axis_index("mp")
        self.x = lax.rem(self.s, NX)
        self.z = lax.rem(self.s // NX, NZ)
        self.h = self.s // PEERS
        self.own = self.s - self.h * PEERS
        self.partner = (self.s, 1 - self.c)
        self.has_self = self.h == self.c

    def group(self, j):
        near = self.z // (NZ // 2)
        zh = (1 - near) if j < 2 else near
        return (j % 2) * 2 + zh

    def peer(self, group, q):
        zz = lax.rem(q // NX + self.z, NZ // 2)
        xx = lax.rem(q + self.x, NX)
        return group * 16 + zz * NX + xx


def greet(me):
    barrier = pltpu.get_barrier_semaphore()

    def one(i, carry):
        peer = lax.rem(me.own + i, PEERS)

        @pl.when(jnp.logical_not(me.has_self & (i == 0)))
        def _():
            pl.semaphore_signal(
                barrier, inc=1, device_id=(me.c * PEERS + peer, me.h), device_id_type=MESH
            )

        return carry

    lax.fori_loop(0, PEERS, one, 0)
    pl.semaphore_signal(barrier, inc=1, device_id=me.partner, device_id_type=MESH)
    return barrier


def await_greetings(me, barrier):
    pl.semaphore_wait(barrier, jnp.where(me.has_self, PEERS, PEERS + 1))


def send_group(me, group, src, dst, at, send_sem, recv_sem):
    landing = pl.multiple_of(at * CELL, CELL)
    mine = me.own // 16

    def one(q, carry):
        peer = me.peer(group, q)
        rows = pl.ds(pl.multiple_of(peer * CELL, CELL), CELL)
        itself = me.has_self & (peer == me.own)

        @pl.when(itself)
        def _():
            pltpu.make_async_copy(
                src.at[rows], dst.at[pl.ds(landing, CELL)], recv_sem.at[mine]
            ).start()

        @pl.when(jnp.logical_not(itself))
        def _():
            pltpu.make_async_remote_copy(
                src_ref=src.at[rows],
                dst_ref=dst.at[pl.ds(landing, CELL)],
                send_sem=send_sem,
                recv_sem=recv_sem.at[mine],
                device_id=(me.c * PEERS + peer, me.h),
                device_id_type=MESH,
            ).start()

        return carry

    lax.fori_loop(0, 16, one, 0)


def await_sends(me, src, dst, send_sem, recv_sem):
    def over(rows):
        pltpu.make_async_remote_copy(
            src_ref=src.at[pl.ds(0, rows)],
            dst_ref=dst.at[pl.ds(0, rows)],
            send_sem=send_sem,
            recv_sem=recv_sem.at[0],
            device_id=me.partner,
            device_id_type=MESH,
        ).wait_send()

    @pl.when(me.has_self)
    def _():
        over(HALF - CELL)

    @pl.when(jnp.logical_not(me.has_self))
    def _():
        over(HALF)


def relay(me, buf, start, rows, send_sem, recv_sem):
    part = buf.at[pl.ds(start, rows)]
    return pltpu.make_async_remote_copy(
        src_ref=part,
        dst_ref=part,
        send_sem=send_sem,
        recv_sem=recv_sem,
        device_id=me.partner,
        device_id_type=MESH,
    )


def local_slots(rank, s):
    return (rank // LENGTH) * CELL + (rank % LENGTH) - s * CELL


WIN = 1152
KEYS = 384
ITEMS = 11


def layer_kernel(
    points, rank, counts, gain_attn, w_qkv, w_out, gain_mlp, w_fc1, w_fc2,
    back,
    send, arrived, wq, wo, f1, f2, kk, marks, vt, qt, ctxv, s0, s1, p0, p1, m0, m1, table,
    send_sem, recv_sem, wloc_sem, wsend_sem, wrecv_sem, ksend_sem, krecv_sem,
    vsend_sem, vrecv_sem, bsend_sem, brecv_sem, rsend_sem, rrecv_sem,
):
    me = Place()
    barrier = greet(me)
    slots = local_slots(rank[...], me.s)
    s_refs, p_refs, m_refs = (s0, s1), (p0, p1), (m0, m1)

    def permute(group):
        first = me.c * HALF + group * GROUP
        total = jnp.zeros((GROUP, FEAT), F32)
        for part in range(4):
            wanted = first + lax.broadcasted_iota(jnp.int32, (GROUP, 512), 0)
            hit = wanted == slots[:, part * 512 : (part + 1) * 512]
            pick = jnp.where(hit, 1.0, 0.0).astype(BF16)
            total = total + dot(pick, points[pl.ds(part * 512, 512), :])
        send[pl.ds(pl.multiple_of(group * GROUP, GROUP), GROUP), :] = total.astype(BF16)

    local, remote = [], []
    for i, (src, dst) in enumerate(((w_qkv, wq), (w_out, wo), (w_fc1, f1), (w_fc2, f2))):
        copy = pltpu.make_async_copy(src, dst.at[me.c], wloc_sem.at[i])
        copy.start()
        local.append(copy)
        remote.append(
            pltpu.make_async_remote_copy(
                src_ref=src,
                dst_ref=dst.at[me.c],
                send_sem=wsend_sem.at[i],
                recv_sem=wrecv_sem.at[i],
                device_id=me.partner,
                device_id_type=MESH,
            )
        )

    for j in range(GROUPS):
        group = me.group(j)
        permute(group)
        if j == 0:
            await_greetings(me, barrier)
            remote[0].start()
        send_group(me, group, send, arrived, me.own, send_sem, recv_sem)
    for copy in remote[1:]:
        copy.start()

    c1 = counts[0, 0]
    c2 = c1 + counts[0, 1]
    c3 = c2 + counts[0, 2]

    def patch_of(position):
        return (
            (position >= c1).astype(jnp.int32)
            + (position >= c2).astype(jnp.int32)
            + (position >= c3).astype(jnp.int32)
        )

    def mark_keys(i, carry):
        patch = patch_of(i * 128 + lax.broadcasted_iota(jnp.int32, (128, 128), 0))
        lane = lax.broadcasted_iota(jnp.int32, (128, 128), 1)
        marks[i] = jnp.where((lane < 4) & (lane != patch), FAR, 0.0).astype(BF16)
        for pair in range(4):
            vt[pair, i, 128:144, :] = jnp.ones((16, 128), BF16)
        return carry

    lax.fori_loop(0, LENGTH // 128, mark_keys, 0)

    def mark_queries(i, carry):
        first = me.c * HALF + i * 128
        patch = patch_of(first + lax.broadcasted_iota(jnp.int32, (128, 256), 1) % 128)
        row = lax.broadcasted_iota(jnp.int32, (128, 256), 0)
        mark = jnp.where(row == patch, 1.0, 0.0).astype(BF16)
        for pair in range(4):
            qt[i, pair, 128:256, :] = mark
        return carry

    lax.fori_loop(0, 8, mark_queries, 0)

    upward = me.z // (NZ // 2)

    def in_stream(n, count):
        return upward * n + (1 - upward) * (count - 1 - n)

    zero = c1 * 0
    firsts, lasts, begins, index = [], [], [], zero
    for n in range(8):
        row = me.c * HALF + in_stream(n, 8) * 128
        firsts.append(patch_of(row))
        lasts.append(patch_of(row + 127))
        begins.append(index)
        index = index + lasts[n] - firsts[n] + 1
        table[2, n] = begins[n]
        table[3, n] = firsts[n]
    for i in range(ITEMS + 1):
        block, patch = in_stream(0, 8), jnp.minimum(firsts[0] + i, lasts[0])
        for n in range(1, 8):
            reached = begins[n] <= i
            block = jnp.where(reached, in_stream(n, 8), block)
            patch = jnp.where(
                reached, jnp.minimum(firsts[n] + i - begins[n], lasts[n]), patch
            )
        start = jnp.where(
            patch >= 3, c3, jnp.where(patch >= 2, c2, jnp.where(patch >= 1, c1, zero))
        )
        table[0, i + 1] = block
        table[1, i + 1] = jnp.minimum(start // 128, (LENGTH - WIN) // 128)

    local[0].wait()
    remote[0].wait_recv()

    def project(group):
        rows = pl.ds(pl.multiple_of(group * GROUP, GROUP), GROUP)
        place = me.c * 8 + group * 2
        normed = norm_rows(arrived[rows, :].astype(F32), gain_attn[...])
        row = lax.broadcasted_iota(jnp.int32, (128, 128), 0)
        for half in range(2):
            keys = dot(normed, wq[half, 1]).astype(BF16)
            values = dot(normed, wq[half, 2])
            for p in range(2):
                pair, cols = 2 * half + p, slice(p * 128, (p + 1) * 128)
                for b in range(2):
                    kk[pair, place + b] = keys[b * 128 : (b + 1) * 128, cols]
                    vt[pair, place + b, 0:128, :] = values[b * 128 : (b + 1) * 128, cols].T.astype(
                        BF16
                    )
        for half in range(2):
            queries = dot(normed, wq[half, 0]) * QSCALE
            for p in range(2):
                pair, cols = 2 * half + p, slice(p * 128, (p + 1) * 128)
                for b in range(2):
                    turned = queries[b * 128 : (b + 1) * 128, cols].T
                    block = group * 2 + b
                    qt[block, pair, 0:128, 0:128] = jnp.where(row < HDIM, turned, 0.0).astype(BF16)
                    qt[block, pair, 0:128, 128:256] = jnp.where(row >= HDIM, turned, 0.0).astype(
                        BF16
                    )

    def exchange(half, group):
        place = half * 8 + group * 2
        k_part = kk.at[:, pl.ds(place, 2)]
        v_part = vt.at[:, pl.ds(place, 2), pl.ds(0, 128)]
        return [
            pltpu.make_async_remote_copy(
                src_ref=part,
                dst_ref=part,
                send_sem=ss.at[group],
                recv_sem=rs.at[group],
                device_id=me.partner,
                device_id_type=MESH,
            )
            for part, ss, rs in (
                (k_part, ksend_sem, krecv_sem),
                (v_part, vsend_sem, vrecv_sem),
            )
        ]

    for j in range(GROUPS):
        group = me.group(j)
        relay(
            me, arrived, pl.multiple_of(group * GROUP, GROUP), GROUP,
            rsend_sem.at[group], recv_sem.at[group],
        ).wait_recv()
        project(group)
        for copy in exchange(me.c, group):
            copy.start()
    await_sends(me, send, arrived, send_sem, recv_sem)
    for i in range(1, 4):
        local[i].wait()
        remote[i].wait_recv()
    for j in range(GROUPS):
        for copy in exchange(1 - me.c, me.group(j)):
            copy.wait_recv()

    def score(pair, item, part, dst, top):
        keys = pl.ds(table[1, item] + part * (KEYS // 128), KEYS // 128)
        lhs = jnp.concatenate([kk[pair, keys], marks[keys]], axis=2).reshape(KEYS, 256)
        value = dot(lhs, qt[table[0, item], pair])
        s_refs[dst][part * KEYS : (part + 1) * KEYS, :] = value
        high = jnp.max(value.reshape(KEYS // 8, 8, 256), axis=0)
        return high if top is None else jnp.maximum(top, high)

    def settle(dst, top):
        m_refs[dst][...] = jnp.broadcast_to(jnp.max(top, axis=0, keepdims=True), (8, 256))

    def raise_part(src, part, top):
        rows = slice(part * 128, (part + 1) * 128)
        p_refs[src][rows, :] = jnp.exp2(s_refs[src][rows, :] - top).astype(BF16)

    def weigh(pair, item, src, low, count, total):
        start = table[1, item] + low // 128
        lhs = [vt[pair, start + b] for b in range(count // 128)]
        lhs = jnp.concatenate(lhs, axis=1) if count > 128 else lhs[0]
        value = dot(lhs, p_refs[src][low : low + count, :])
        return value if total is None else total + value

    def conclude(pair, item, total):
        inverse = 1.0 / total[128:129, :]
        result = jnp.concatenate(
            [
                total[0:64, 0:128] * inverse[:, 0:128],
                total[64:128, 128:256] * inverse[:, 128:256],
            ],
            axis=0,
        )
        ctxv[item, :, pair * 128 : (pair + 1) * 128] = result.T.astype(BF16)

    def step(item, pair):
        now, other = pair % 2, 1 - pair % 2
        after, after_pair = (item, pair + 1) if pair < 3 else (item + 1, 0)
        before, before_pair = (item, pair - 1) if pair > 0 else (item - 1, 3)
        top = m_refs[now][0:1, :]
        high = total = None
        for part in range(9):
            if part % 3 == 0:
                high = score(after_pair, after, part // 3, other, high)
            raise_part(now, part, top)
            if part % 2 == 1:
                total = weigh(before_pair, before, other, (part - 1) * 128, 256, total)
        total = weigh(before_pair, before, other, 1024, 128, total)
        conclude(before_pair, before, total)
        settle(other, high)

    def one_item(item, carry):
        for pair in range(4):
            step(item, pair)
        return carry

    table[0, 0] = table[0, 1]
    table[1, 0] = table[1, 1]
    p1[...] = jnp.zeros_like(p1)
    high = None
    for part in range(3):
        high = score(0, 1, part, 0, high)
    settle(0, high)

    def block_context(n):
        begin, first = table[2, n] + 1, table[3, n]
        row = me.c * HALF + in_stream(n, 8) * 128
        nth = patch_of(row + lax.broadcasted_iota(jnp.int32, (128, FEAT), 0)) - first
        value = ctxv[begin]
        for e in range(1, 4):
            value = jnp.where(nth >= e, ctxv[jnp.minimum(begin + e, ITEMS)], value)
        return value

    def finish(j):
        group = in_stream(j, GROUPS)
        low, high = 2 * j + 1 - upward, 2 * j + upward
        ctx = jnp.concatenate([block_context(low), block_context(high)], axis=0)
        rows = pl.ds(pl.multiple_of(group * GROUP, GROUP), GROUP)
        attn = dot(ctx[:, :256], wo[0]) + dot(ctx[:, 256:], wo[1])
        middle = (arrived[rows, :].astype(F32) + attn.astype(BF16).astype(F32)).astype(BF16)
        middle = middle.astype(F32)
        normed = norm_rows(middle, gain_mlp[...])
        result = middle
        for half in range(2):
            hidden = jax.nn.gelu(dot(normed, f1[half]), approximate=True).astype(BF16)
            result = result + dot(hidden, f2[half])
        send[rows, :] = result.astype(BF16)
        send_group(me, group, send, back, me.s, bsend_sem, brecv_sem)

    def stretch(j, carry):
        low = jnp.where(j == 0, 1, 2 * j + 4)
        high = 2 * j + 6
        lax.fori_loop(low, high, one_item, 0)
        total = None
        for part in range(4):
            total = weigh(3, high - 1, 1, part * 256, 256, total)
        conclude(3, high - 1, weigh(3, high - 1, 1, 1024, 128, total))
        finish(j)
        return carry

    lax.fori_loop(0, GROUPS, stretch, 0)

    early = jnp.where(me.own // 16 < 2, 1, 0)
    order = [early, early + 2, 1 - early, 3 - early]

    def passing(half, group, recv):
        start = pl.multiple_of(half * HALF + group * GROUP, GROUP)
        return relay(me, back, start, GROUP, rsend_sem.at[group], recv.at[group])

    for group in order:
        passing(me.c, group, brecv_sem).wait_recv()
        passing(me.c, group, rrecv_sem).start()
    for group in order:
        passing(1 - me.c, group, rrecv_sem).wait_recv()
    for group in order:
        passing(me.c, group, rrecv_sem).wait_send()
    await_sends(me, send, back, bsend_sem, brecv_sem)
    for j in range(GROUPS):
        for copy in exchange(me.c, me.group(j)):
            copy.wait_send()
    for copy in remote:
        copy.wait_send()


def place_kernel(rank, back, out):
    s = lax.axis_index("space")
    i = pl.program_id(0)
    slots = local_slots(rank[...], s)
    total = jnp.zeros((256, FEAT), F32)
    columns = [
        jnp.broadcast_to(slots[:, p * 128 : (p + 1) * 128], (128, 128)).T for p in range(2)
    ]
    column = jnp.concatenate(columns, axis=0)
    lane = lax.broadcasted_iota(jnp.int32, (256, 128), 1)
    for part in range(4):
        picks = [
            jnp.where(column == lane + (part * 512 + t * 128), 1.0, 0.0).astype(BF16)
            for t in range(4)
        ]
        total = total + dot(jnp.concatenate(picks, axis=1), back[pl.ds(part * 512, 512), :])
    out[...] = total.astype(BF16)


def body(
    points, curve_rank, patch_counts, norm_gain_attn, w_qkv, w_out, norm_gain_mlp, w_fc1, w_fc2
):
    rank = curve_rank.reshape(1, LENGTH)
    shape = jax.ShapeDtypeStruct
    vm = pl.BlockSpec(memory_space=pltpu.VMEM)
    anywhere = pl.BlockSpec(memory_space=pl.ANY)
    dma = pltpu.SemaphoreType.DMA
    back = pl.pallas_call(
        layer_kernel,
        name="layer",
        out_shape=shape((LENGTH, FEAT), BF16),
        in_specs=[vm, vm, pl.BlockSpec(memory_space=pltpu.SMEM), vm, anywhere, anywhere, vm]
        + [anywhere] * 2,
        out_specs=vm,
        scratch_shapes=[
            VMEM((HALF, FEAT), BF16),
            VMEM((HALF, FEAT), BF16),
            VMEM((2,) + w_qkv.shape, BF16),
            VMEM((2,) + w_out.shape, BF16),
            VMEM((2,) + w_fc1.shape, BF16),
            VMEM((2,) + w_fc2.shape, BF16),
            VMEM((4, 16, 128, 128), BF16),
            VMEM((16, 128, 128), BF16),
            VMEM((4, 16, 144, 128), BF16),
            VMEM((8, 4, 256, 256), BF16),
            VMEM((ITEMS + 1, 128, FEAT), BF16),
            VMEM((WIN, 256), F32),
            VMEM((WIN, 256), F32),
            VMEM((WIN, 256), BF16),
            VMEM((WIN, 256), BF16),
            VMEM((8, 256), F32),
            VMEM((8, 256), F32),
            pltpu.SMEM((4, 16), jnp.int32),
            dma, dma((4,)), dma((4,)), dma((4,)), dma((4,)), dma((4,)), dma((4,)),
            dma((4,)), dma((4,)), dma, dma((4,)), dma((4,)), dma((4,)),
        ],
        compiler_params=pltpu.CompilerParams(collective_id=0, has_side_effects=True),
    )(
        points, rank, patch_counts, norm_gain_attn.reshape(1, FEAT), w_qkv, w_out,
        norm_gain_mlp.reshape(1, FEAT), w_fc1, w_fc2,
    )

    return pl.pallas_call(
        place_kernel,
        name="place_rows",
        grid=(LENGTH // 256,),
        out_shape=shape((LENGTH, FEAT), BF16),
        in_specs=[
            pl.BlockSpec((1, 256), lambda i: (0, i)),
            pl.BlockSpec((LENGTH, FEAT), lambda i: (0, 0)),
        ],
        out_specs=pl.BlockSpec((256, FEAT), lambda i: (i, 0)),
    )(rank, back)


def solution(mesh):
    placed = (
        P("space", None),
        P("space"),
        P("space", None),
        P(),
        P(None, None, "mp"),
        P("mp", None),
        P(),
        P(None, "mp"),
        P("mp", None),
    )
    return jax.shard_map(
        body, mesh=mesh, in_specs=placed, out_specs=P("space", None), check_vma=False
    )
```

time: 129 us -> 95.6 us (0.74)
  the two profiles are of different devices: /device:TPU:73 before, /device:TPU:97 now
where the time goes in v2:
time: 95.6 us; the launch traced here: 95.1 us
  Pallas kernels  95.1 us (99%)
    pallas_call x1, Pallas kernels, body(): pl.pallas_call(layer_kernel, name='layer', out_shape=shape((LENGTH, FEAT)...  86.6 us
    pallas_call x1, Pallas kernels, body(): pl.pallas_call(place_kernel, name='place_rows', grid=(LENGTH // 256,), ou...  8.49 us

profile of v2, /device:TPU:97, one launch (start us, length us, event | category | flops | bytes accessed | tf_op | source)
XLA Modules:
  0.0 95.1 jit_solution(7843821628554972143)
XLA Ops:
  0.0 86.6 %layer.1.back = bf16[2048,512]{1,0:T(8,128)(2,1)} custom-call(bf16[2048,512]{1,0:T(8,128)(2,1)} %points.1, s32[1,2048]{1,0:T(1,128)} %bitcast.3, s32[1,4]{1,0:T(1,128)} %counts.1, f32[1,512]{1,0:T(1,128)} %bitcast.5, bf16[3,512,256]{2,1,0:T(8,128)(2,1)} %w_qkv.1, bf16[256,512]{1,0:T(8,128)(2,1)} %w_out.1, f32[1,512]{1,0:T(1,128)} %bitcast.6, ...), custom_call_target="tpu_custom_call" | custom-call | tf_op jit(solution)/shard_map/layer/pallas_call | solution.py:484
  86.6 8.5 %place_rows.1 = bf16[2048,512]{1,0:T(8,128)(2,1)} custom-call(s32[1,2048]{1,0:T(1,128)} %bitcast.4, bf16[2048,512]{1,0:T(8,128)(2,1)} %layer.1.back), custom_call_target="tpu_custom_call" | custom-call | tf_op jit(solution)/shard_map/place_rows/pallas_call | solution.py:519

commit v3 on v2

--- a/solution.py
+++ b/solution.py
@@ -152,6 +152,39 @@
     return (rank // LENGTH) * CELL + (rank % LENGTH) - s * CELL
 
 
+def early_groups(me):
+    return jnp.where(me.own // 16 < 2, 1, 0)
+
+
+def group_bases(parity):
+    return [
+        pl.multiple_of(half * HALF + (parity + 2 * k) * GROUP, GROUP)
+        for half in range(2)
+        for k in range(2)
+    ]
+
+
+def slot_column(slots):
+    return jnp.concatenate(
+        [
+            jnp.broadcast_to(slots[:, p * 128 : (p + 1) * 128], (128, 128)).T
+            for p in range(slots.shape[1] // 128)
+        ],
+        axis=0,
+    )
+
+
+def picks(column, base):
+    lane = lax.broadcasted_iota(jnp.int32, column.shape, 1)
+    return jnp.concatenate(
+        [
+            jnp.where(column == lane + (base + t * 128), 1.0, 0.0).astype(BF16)
+            for t in range(GROUP // 128)
+        ],
+        axis=1,
+    )
+
+
 WIN = 1152
 KEYS = 384
 ITEMS = 11
@@ -159,10 +192,11 @@
 
 def layer_kernel(
     points, rank, counts, gain_attn, w_qkv, w_out, gain_mlp, w_fc1, w_fc2,
-    back,
-    send, arrived, wq, wo, f1, f2, kk, marks, vt, qt, ctxv, s0, s1, p0, p1, m0, m1, table,
+    part_ref, late_ref,
+    back, placed, send, arrived, wq, wo, f1, f2, kk, marks, vt, qt, ctxv, s0, s1, p0, p1, m0, m1, table,
     send_sem, recv_sem, wloc_sem, wsend_sem, wrecv_sem, ksend_sem, krecv_sem,
     vsend_sem, vrecv_sem, bsend_sem, brecv_sem, rsend_sem, rrecv_sem,
+    out_sem,
 ):
     me = Place()
     barrier = greet(me)
@@ -315,7 +349,7 @@
             )
         ]
 
-    for j in range(GROUPS):
+    for j in (2, 3, 0, 1):
         group = me.group(j)
         relay(
             me, arrived, pl.multiple_of(group * GROUP, GROUP), GROUP,
@@ -324,10 +358,6 @@
         project(group)
         for copy in exchange(me.c, group):
             copy.start()
-    await_sends(me, send, arrived, send_sem, recv_sem)
-    for i in range(1, 4):
-        local[i].wait()
-        remote[i].wait_recv()
     for j in range(GROUPS):
         for copy in exchange(1 - me.c, me.group(j)):
             copy.wait_recv()
@@ -427,25 +457,58 @@
         for part in range(4):
             total = weigh(3, high - 1, 1, part * 256, 256, total)
         conclude(3, high - 1, weigh(3, high - 1, 1, 1024, 128, total))
+
+        @pl.when(j == 0)
+        def _():
+            await_sends(me, send, arrived, send_sem, recv_sem)
+            for i in range(1, 4):
+                local[i].wait()
+                remote[i].wait_recv()
+
         finish(j)
         return carry
 
     lax.fori_loop(0, GROUPS, stretch, 0)
 
-    early = jnp.where(me.own // 16 < 2, 1, 0)
-    order = [early, early + 2, 1 - early, 3 - early]
+    early = early_groups(me)
 
     def passing(half, group, recv):
         start = pl.multiple_of(half * HALF + group * GROUP, GROUP)
         return relay(me, back, start, GROUP, rsend_sem.at[group], recv.at[group])
 
-    for group in order:
-        passing(me.c, group, brecv_sem).wait_recv()
-        passing(me.c, group, rrecv_sem).start()
-    for group in order:
-        passing(1 - me.c, group, rrecv_sem).wait_recv()
-    for group in order:
+    def hand_on(groups):
+        for group in groups:
+            passing(me.c, group, brecv_sem).wait_recv()
+            passing(me.c, group, rrecv_sem).start()
+        for group in groups:
+            passing(1 - me.c, group, rrecv_sem).wait_recv()
+
+    hand_on([early, early + 2])
+
+    def place_early(i, carry):
+        rows = pl.ds(pl.multiple_of(i * 256, 256), 256)
+        column = slot_column(local_slots(rank[:, rows], me.s))
+        total = None
+        for base in group_bases(early):
+            value = dot(picks(column, base), back[pl.ds(base, GROUP), :])
+            total = value if total is None else total + value
+        placed[rows, :] = total.astype(BF16)
+        return carry
+
+    lax.fori_loop(0, LENGTH // 256, place_early, 0)
+    outs = [pltpu.make_async_copy(placed, part_ref, out_sem.at[4])]
+    outs[0].start()
+    hand_on([1 - early, 3 - early])
+    for i, base in enumerate(group_bases(1 - early)):
+        copy = pltpu.make_async_copy(
+            back.at[pl.ds(base, GROUP)], late_ref.at[pl.ds(i * GROUP, GROUP)], out_sem.at[i]
+        )
+        copy.start()
+        outs.append(copy)
+    for group in (early, early + 2, 1 - early, 3 - early):
         passing(me.c, group, rrecv_sem).wait_send()
+    for copy in outs:
+        copy.wait()
     await_sends(me, send, back, bsend_sem, brecv_sem)
     for j in range(GROUPS):
         for copy in exchange(me.c, me.group(j)):
@@ -454,22 +517,12 @@
         copy.wait_send()
 
 
-def place_kernel(rank, back, out):
-    s = lax.axis_index("space")
-    i = pl.program_id(0)
-    slots = local_slots(rank[...], s)
-    total = jnp.zeros((256, FEAT), F32)
-    columns = [
-        jnp.broadcast_to(slots[:, p * 128 : (p + 1) * 128], (128, 128)).T for p in range(2)
-    ]
-    column = jnp.concatenate(columns, axis=0)
-    lane = lax.broadcasted_iota(jnp.int32, (256, 128), 1)
-    for part in range(4):
-        picks = [
-            jnp.where(column == lane + (part * 512 + t * 128), 1.0, 0.0).astype(BF16)
-            for t in range(4)
-        ]
-        total = total + dot(jnp.concatenate(picks, axis=1), back[pl.ds(part * 512, 512), :])
+def place_kernel(rank, part, late, out):
+    me = Place()
+    column = slot_column(local_slots(rank[...], me.s))
+    total = part[...].astype(F32)
+    for i, base in enumerate(group_bases(1 - early_groups(me))):
+        total = total + dot(picks(column, base), late[pl.ds(i * GROUP, GROUP), :])
     out[...] = total.astype(BF16)
 
 
@@ -481,14 +534,16 @@
     vm = pl.BlockSpec(memory_space=pltpu.VMEM)
     anywhere = pl.BlockSpec(memory_space=pl.ANY)
     dma = pltpu.SemaphoreType.DMA
-    back = pl.pallas_call(
+    part, late = pl.pallas_call(
         layer_kernel,
         name="layer",
-        out_shape=shape((LENGTH, FEAT), BF16),
+        out_shape=(shape((LENGTH, FEAT), BF16), shape((HALF, FEAT), BF16)),
         in_specs=[vm, vm, pl.BlockSpec(memory_space=pltpu.SMEM), vm, anywhere, anywhere, vm]
         + [anywhere] * 2,
-        out_specs=vm,
+        out_specs=[anywhere] * 2,
         scratch_shapes=[
+            VMEM((LENGTH, FEAT), BF16),
+            VMEM((LENGTH, FEAT), BF16),
             VMEM((HALF, FEAT), BF16),
             VMEM((HALF, FEAT), BF16),
             VMEM((2,) + w_qkv.shape, BF16),
@@ -508,7 +563,7 @@
             VMEM((8, 256), F32),
             pltpu.SMEM((4, 16), jnp.int32),
             dma, dma((4,)), dma((4,)), dma((4,)), dma((4,)), dma((4,)), dma((4,)),
-            dma((4,)), dma((4,)), dma, dma((4,)), dma((4,)), dma((4,)),
+            dma((4,)), dma((4,)), dma, dma((4,)), dma((4,)), dma((4,)), dma((5,)),
         ],
         compiler_params=pltpu.CompilerParams(collective_id=0, has_side_effects=True),
     )(
@@ -519,14 +574,15 @@
     return pl.pallas_call(
         place_kernel,
         name="place_rows",
-        grid=(LENGTH // 256,),
+        grid=(LENGTH // 1024,),
         out_shape=shape((LENGTH, FEAT), BF16),
         in_specs=[
-            pl.BlockSpec((1, 256), lambda i: (0, i)),
-            pl.BlockSpec((LENGTH, FEAT), lambda i: (0, 0)),
+            pl.BlockSpec((1, 1024), lambda i: (0, i)),
+            pl.BlockSpec((1024, FEAT), lambda i: (i, 0)),
+            pl.BlockSpec((HALF, FEAT), lambda i: (0, 0)),
         ],
-        out_specs=pl.BlockSpec((256, FEAT), lambda i: (i, 0)),
-    )(rank, back)
+        out_specs=pl.BlockSpec((1024, FEAT), lambda i: (i, 0)),
+    )(rank, part, late)
 
 
 def solution(mesh):

time: 95.6 us -> 92 us (0.962)
  Pallas kernels: 95.1 us -> 91.9 us
    pallas_call x2, Pallas kernels: 95.1 us -> 91.9 us  [the longest x1 86.7 us: body(): pl.pallas_call(layer_kernel, name='layer', out_shape=(shape((LENGTH, FEAT...]
where the time goes in v3:
time: 92 us; the launch traced here: 91.9 us
  Pallas kernels  91.9 us (100%)
    pallas_call x1, Pallas kernels, body(): pl.pallas_call(layer_kernel, name='layer', out_shape=(shape((LENGTH, FEAT...  86.7 us
    pallas_call x1, Pallas kernels, body(): pl.pallas_call(place_kernel, name='place_rows', grid=(LENGTH // 1024,), o...  5.18 us

profile of v3, /device:TPU:97, one launch (start us, length us, event | category | flops | bytes accessed | tf_op | source)
XLA Modules:
  0.0 91.9 jit_solution(725224093437498939)
XLA Ops:
  0.0 86.7 %layer.1 = (bf16[2048,512]{1,0:T(8,128)(2,1)}, bf16[1024,512]{1,0:T(8,128)(2,1)}) custom-call(bf16[2048,512]{1,0:T(8,128)(2,1)} %points.1, s32[1,2048]{1,0:T(1,128)} %bitcast.3, s32[1,4]{1,0:T(1,128)} %counts.1, f32[1,512]{1,0:T(1,128)} %bitcast.5, bf16[3,512,256]{2,1,0:T(8,128)(2,1)} %w_qkv.1, bf16[256,512]{1,0:T(8,128)(2,1)} %w_out.1, f32[1,512]{1,0:T(1,128)} %bitcast.6, ...), custom_call_target="tpu_custom_call" | custom-call | tf_op jit(solution)/shard_map/layer/pallas_call | solution.py:537
  86.7 5.2 %place_rows.1 = bf16[2048,512]{1,0:T(8,128)(2,1)} custom-call(s32[1,2048]{1,0:T(1,128)} %bitcast.4, bf16[2048,512]{1,0:T(8,128)(2,1)} %get-tuple-element.7.part, bf16[1024,512]{1,0:T(8,128)(2,1)} %get-tuple-element.8.late), custom_call_target="tpu_custom_call" | custom-call | tf_op jit(solution)/shard_map/place_rows/pallas_call | solution.py:574

commit v4 on v3

--- a/solution.py
+++ b/solution.py
@@ -48,18 +48,22 @@
         self.z = lax.rem(self.s // NX, NZ)
         self.h = self.s // PEERS
         self.own = self.s - self.h * PEERS
+        self.y = self.own // 32
         self.partner = (self.s, 1 - self.c)
         self.has_self = self.h == self.c
 
     def group(self, j):
         near = self.z // (NZ // 2)
-        zh = (1 - near) if j < 2 else near
-        return (j % 2) * 2 + zh
-
-    def peer(self, group, q):
-        zz = lax.rem(q // NX + self.z, NZ // 2)
+        zh = jnp.where(j < 2, 1 - near, near)
+        return lax.rem(self.y + j, 2) * 2 + zh
+
+    def block(self, n):
+        return self.group(n // 2) * 2 + n % 2
+
+    def peer(self, first, count, q):
+        zz = lax.rem(q // NX + self.z, count // NX)
         xx = lax.rem(q + self.x, NX)
-        return group * 16 + zz * NX + xx
+        return first + zz * NX + xx
 
 
 def greet(me):
@@ -85,12 +89,12 @@
     pl.semaphore_wait(barrier, jnp.where(me.has_self, PEERS, PEERS + 1))
 
 
-def send_group(me, group, src, dst, at, send_sem, recv_sem):
+def send_cells(me, first, count, src, dst, at, send_sem, recv_sem):
     landing = pl.multiple_of(at * CELL, CELL)
     mine = me.own // 16
 
     def one(q, carry):
-        peer = me.peer(group, q)
+        peer = me.peer(first, count, q)
         rows = pl.ds(pl.multiple_of(peer * CELL, CELL), CELL)
         itself = me.has_self & (peer == me.own)
 
@@ -113,7 +117,7 @@
 
         return carry
 
-    lax.fori_loop(0, 16, one, 0)
+    lax.fori_loop(0, count, one, 0)
 
 
 def await_sends(me, src, dst, send_sem, recv_sem):
@@ -152,13 +156,9 @@
     return (rank // LENGTH) * CELL + (rank % LENGTH) - s * CELL
 
 
-def early_groups(me):
-    return jnp.where(me.own // 16 < 2, 1, 0)
-
-
-def group_bases(parity):
+def group_bases(y):
     return [
-        pl.multiple_of(half * HALF + (parity + 2 * k) * GROUP, GROUP)
+        pl.multiple_of(half * HALF + (2 * y + k) * GROUP, GROUP)
         for half in range(2)
         for k in range(2)
     ]
@@ -191,15 +191,30 @@
 
 
 def layer_kernel(
-    points, rank, counts, gain_attn, w_qkv, w_out, gain_mlp, w_fc1, w_fc2,
-    part_ref, late_ref,
+    points_in, rank_in, counts_in, gain_attn_in, w_qkv, w_out, gain_mlp_in, w_fc1, w_fc2,
+    part_ref, late_ref, points, rank, counts, gain_attn, gain_mlp,
     back, placed, send, arrived, wq, wo, f1, f2, kk, marks, vt, qt, ctxv, s0, s1, p0, p1, m0, m1, table,
     send_sem, recv_sem, wloc_sem, wsend_sem, wrecv_sem, ksend_sem, krecv_sem,
     vsend_sem, vrecv_sem, bsend_sem, brecv_sem, rsend_sem, rrecv_sem,
-    out_sem,
+    out_sem, load_sem,
 ):
     me = Place()
     barrier = greet(me)
+    loads = [
+        pltpu.make_async_copy(src, dst, load_sem.at[i])
+        for i, (src, dst) in enumerate(
+            (
+                (rank_in, rank),
+                (points_in, points),
+                (counts_in, counts),
+                (gain_attn_in, gain_attn),
+                (gain_mlp_in, gain_mlp),
+            )
+        )
+    ]
+    for copy in loads:
+        copy.start()
+    loads[0].wait()
     slots = local_slots(rank[...], me.s)
     s_refs, p_refs, m_refs = (s0, s1), (p0, p1), (m0, m1)
 
@@ -229,15 +244,19 @@
             )
         )
 
+    loads[1].wait()
     for j in range(GROUPS):
         group = me.group(j)
         permute(group)
         if j == 0:
             await_greetings(me, barrier)
             remote[0].start()
-        send_group(me, group, send, arrived, me.own, send_sem, recv_sem)
+        send_cells(me, group * 16, 16, send, arrived, me.own, send_sem, recv_sem)
     for copy in remote[1:]:
         copy.start()
+
+    for copy in loads[2:]:
+        copy.wait()
 
     c1 = counts[0, 0]
     c2 = c1 + counts[0, 1]
@@ -271,15 +290,10 @@
 
     lax.fori_loop(0, 8, mark_queries, 0)
 
-    upward = me.z // (NZ // 2)
-
-    def in_stream(n, count):
-        return upward * n + (1 - upward) * (count - 1 - n)
-
     zero = c1 * 0
     firsts, lasts, begins, index = [], [], [], zero
     for n in range(8):
-        row = me.c * HALF + in_stream(n, 8) * 128
+        row = me.c * HALF + me.block(n) * 128
         firsts.append(patch_of(row))
         lasts.append(patch_of(row + 127))
         begins.append(index)
@@ -287,10 +301,10 @@
         table[2, n] = begins[n]
         table[3, n] = firsts[n]
     for i in range(ITEMS + 1):
-        block, patch = in_stream(0, 8), jnp.minimum(firsts[0] + i, lasts[0])
+        block, patch = me.block(0), jnp.minimum(firsts[0] + i, lasts[0])
         for n in range(1, 8):
             reached = begins[n] <= i
-            block = jnp.where(reached, in_stream(n, 8), block)
+            block = jnp.where(reached, me.block(n), block)
             patch = jnp.where(
                 reached, jnp.minimum(firsts[n] + i - begins[n], lasts[n]), patch
             )
@@ -349,7 +363,7 @@
             )
         ]
 
-    for j in (2, 3, 0, 1):
+    for j in (0, 2, 3, 1):
         group = me.group(j)
         relay(
             me, arrived, pl.multiple_of(group * GROUP, GROUP), GROUP,
@@ -426,18 +440,18 @@
 
     def block_context(n):
         begin, first = table[2, n] + 1, table[3, n]
-        row = me.c * HALF + in_stream(n, 8) * 128
+        row = me.c * HALF + me.block(n) * 128
         nth = patch_of(row + lax.broadcasted_iota(jnp.int32, (128, FEAT), 0)) - first
         value = ctxv[begin]
         for e in range(1, 4):
             value = jnp.where(nth >= e, ctxv[jnp.minimum(begin + e, ITEMS)], value)
         return value
 
-    def finish(j):
-        group = in_stream(j, GROUPS)
-        low, high = 2 * j + 1 - upward, 2 * j + upward
-        ctx = jnp.concatenate([block_context(low), block_context(high)], axis=0)
-        rows = pl.ds(pl.multiple_of(group * GROUP, GROUP), GROUP)
+    def finish(n, blocks):
+        ctx = [block_context(n + b) for b in range(blocks)]
+        ctx = jnp.concatenate(ctx, axis=0) if blocks > 1 else ctx[0]
+        block = me.block(n)
+        rows = pl.ds(pl.multiple_of(block * 128, 128), blocks * 128)
         attn = dot(ctx[:, :256], wo[0]) + dot(ctx[:, 256:], wo[1])
         middle = (arrived[rows, :].astype(F32) + attn.astype(BF16).astype(F32)).astype(BF16)
         middle = middle.astype(F32)
@@ -447,30 +461,35 @@
             hidden = jax.nn.gelu(dot(normed, f1[half]), approximate=True).astype(BF16)
             result = result + dot(hidden, f2[half])
         send[rows, :] = result.astype(BF16)
-        send_group(me, group, send, back, me.s, bsend_sem, brecv_sem)
-
-    def stretch(j, carry):
-        low = jnp.where(j == 0, 1, 2 * j + 4)
-        high = 2 * j + 6
+        send_cells(me, block * 8, blocks * 8, send, back, me.s, bsend_sem, brecv_sem)
+
+    def stretch(k, carry):
+        low = jnp.where(k == 0, 1, jnp.where(k == 1, 5, 2 * k + 2))
+        high = jnp.where(k == 0, 5, 2 * k + 4)
         lax.fori_loop(low, high, one_item, 0)
         total = None
         for part in range(4):
             total = weigh(3, high - 1, 1, part * 256, 256, total)
         conclude(3, high - 1, weigh(3, high - 1, 1, 1024, 128, total))
 
-        @pl.when(j == 0)
+        @pl.when(k == 0)
         def _():
             await_sends(me, send, arrived, send_sem, recv_sem)
             for i in range(1, 4):
                 local[i].wait()
                 remote[i].wait_recv()
 
-        finish(j)
+        @pl.when(k < 2)
+        def _():
+            finish(k, 1)
+
+        @pl.when(k >= 2)
+        def _():
+            finish(2 * k - 2, 2)
+
         return carry
 
-    lax.fori_loop(0, GROUPS, stretch, 0)
-
-    early = early_groups(me)
+    lax.fori_loop(0, GROUPS + 1, stretch, 0)
 
     def passing(half, group, recv):
         start = pl.multiple_of(half * HALF + group * GROUP, GROUP)
@@ -483,13 +502,13 @@
         for group in groups:
             passing(1 - me.c, group, rrecv_sem).wait_recv()
 
-    hand_on([early, early + 2])
+    hand_on([me.group(0), me.group(2)])
 
     def place_early(i, carry):
         rows = pl.ds(pl.multiple_of(i * 256, 256), 256)
         column = slot_column(local_slots(rank[:, rows], me.s))
         total = None
-        for base in group_bases(early):
+        for base in group_bases(me.y):
             value = dot(picks(column, base), back[pl.ds(base, GROUP), :])
             total = value if total is None else total + value
         placed[rows, :] = total.astype(BF16)
@@ -498,14 +517,14 @@
     lax.fori_loop(0, LENGTH // 256, place_early, 0)
     outs = [pltpu.make_async_copy(placed, part_ref, out_sem.at[4])]
     outs[0].start()
-    hand_on([1 - early, 3 - early])
-    for i, base in enumerate(group_bases(1 - early)):
+    hand_on([me.group(3), me.group(1)])
+    for i, base in enumerate(group_bases(1 - me.y)):
         copy = pltpu.make_async_copy(
             back.at[pl.ds(base, GROUP)], late_ref.at[pl.ds(i * GROUP, GROUP)], out_sem.at[i]
         )
         copy.start()
         outs.append(copy)
-    for group in (early, early + 2, 1 - early, 3 - early):
+    for group in range(GROUPS):
         passing(me.c, group, rrecv_sem).wait_send()
     for copy in outs:
         copy.wait()
@@ -521,7 +540,7 @@
     me = Place()
     column = slot_column(local_slots(rank[...], me.s))
     total = part[...].astype(F32)
-    for i, base in enumerate(group_bases(1 - early_groups(me))):
+    for i, base in enumerate(group_bases(1 - me.y)):
         total = total + dot(picks(column, base), late[pl.ds(i * GROUP, GROUP), :])
     out[...] = total.astype(BF16)
 
@@ -538,10 +557,14 @@
         layer_kernel,
         name="layer",
         out_shape=(shape((LENGTH, FEAT), BF16), shape((HALF, FEAT), BF16)),
-        in_specs=[vm, vm, pl.BlockSpec(memory_space=pltpu.SMEM), vm, anywhere, anywhere, vm]
-        + [anywhere] * 2,
+        in_specs=[anywhere] * 9,
         out_specs=[anywhere] * 2,
         scratch_shapes=[
+            VMEM((LENGTH, FEAT), BF16),
+            VMEM((1, LENGTH), jnp.int32),
+            pltpu.SMEM((1, 4), jnp.int32),
+            VMEM((1, FEAT), F32),
+            VMEM((1, FEAT), F32),
             VMEM((LENGTH, FEAT), BF16),
             VMEM((LENGTH, FEAT), BF16),
             VMEM((HALF, FEAT), BF16),
@@ -563,7 +586,7 @@
             VMEM((8, 256), F32),
             pltpu.SMEM((4, 16), jnp.int32),
             dma, dma((4,)), dma((4,)), dma((4,)), dma((4,)), dma((4,)), dma((4,)),
-            dma((4,)), dma((4,)), dma, dma((4,)), dma((4,)), dma((4,)), dma((5,)),
+            dma((4,)), dma((4,)), dma, dma((4,)), dma((4,)), dma((4,)), dma((5,)), dma((5,)),
         ],
         compiler_params=pltpu.CompilerParams(collective_id=0, has_side_effects=True),
     )(

time: 92 us -> 90.4 us (0.983)
  Pallas kernels: 91.9 us -> 89.4 us
    pallas_call x1, Pallas kernels: 86.7 us -> 84.2 us  [body(): pl.pallas_call(layer_kernel, name='layer', out_shape=(shape((LENGTH, FEAT...]
where the time goes in v4:
time: 90.4 us; the launch traced here: 89.4 us
  Pallas kernels  89.4 us (99%)
    pallas_call x1, Pallas kernels, body(): pl.pallas_call(layer_kernel, name='layer', out_shape=(shape((LENGTH, FEAT...  84.2 us
    pallas_call x1, Pallas kernels, body(): pl.pallas_call(place_kernel, name='place_rows', grid=(LENGTH // 1024,), o...  5.18 us

profile of v4, /device:TPU:97, one launch (start us, length us, event | category | flops | bytes accessed | tf_op | source)
XLA Modules:
  0.0 89.4 jit_solution(13367328272405899472)
XLA Ops:
  0.0 84.2 %layer.1 = (bf16[2048,512]{1,0:T(8,128)(2,1)}, bf16[1024,512]{1,0:T(8,128)(2,1)}) custom-call(bf16[2048,512]{1,0:T(8,128)(2,1)} %points_in.1, s32[1,2048]{1,0:T(1,128)} %bitcast.3, s32[1,4]{1,0:T(1,128)} %counts_in.1, f32[1,512]{1,0:T(1,128)} %bitcast.5, bf16[3,512,256]{2,1,0:T(8,128)(2,1)} %w_qkv.1, bf16[256,512]{1,0:T(8,128)(2,1)} %w_out.1, ...), custom_call_target="tpu_custom_call" | custom-call | tf_op jit(solution)/shard_map/layer/pallas_call | solution.py:556
  84.2 5.2 %place_rows.1 = bf16[2048,512]{1,0:T(8,128)(2,1)} custom-call(s32[1,2048]{1,0:T(1,128)} %bitcast.4, bf16[2048,512]{1,0:T(8,128)(2,1)} %get-tuple-element.7.part, bf16[1024,512]{1,0:T(8,128)(2,1)} %get-tuple-element.8.late), custom_call_target="tpu_custom_call" | custom-call | tf_op jit(solution)/shard_map/place_rows/pallas_call | solution.py:597

commit v5 on v4

--- a/solution.py
+++ b/solution.py
@@ -60,27 +60,36 @@
     def block(self, n):
         return self.group(n // 2) * 2 + n % 2
 
-    def peer(self, first, count, q):
-        zz = lax.rem(q // NX + self.z, count // NX)
-        xx = lax.rem(q + self.x, NX)
-        return first + zz * NX + xx
+    def peers(self, first, count):
+        rows = [lax.rem(self.z + i, count // NX) * NX + first for i in range(count // NX)]
+        places = [lax.rem(self.x + i, NX) for i in range(NX)]
+        return [rows[q // NX] + places[q % NX] for q in range(count)]
 
 
 def greet(me):
     barrier = pltpu.get_barrier_semaphore()
 
+    places = [lax.rem(me.x + i, NX) for i in (2, 1, 3, 0)]
+
     def one(i, carry):
-        peer = lax.rem(me.own + i, PEERS)
-
-        @pl.when(jnp.logical_not(me.has_self & (i == 0)))
-        def _():
-            pl.semaphore_signal(
-                barrier, inc=1, device_id=(me.c * PEERS + peer, me.h), device_id_type=MESH
-            )
+        away = NZ // 2 + (i + 1) // 2 * (2 * lax.rem(i, 2) - 1)
+        first = lax.rem(me.z + away, NZ) * NX
+        for y in range(2):
+            for place in places:
+                peer = first + (y * NZ * NX + place)
+
+                @pl.when(jnp.logical_not(me.has_self & (peer == me.own)))
+                def _():
+                    pl.semaphore_signal(
+                        barrier,
+                        inc=1,
+                        device_id=(me.c * PEERS + peer, me.h),
+                        device_id_type=MESH,
+                    )
 
         return carry
 
-    lax.fori_loop(0, PEERS, one, 0)
+    lax.fori_loop(0, NZ, one, 0)
     pl.semaphore_signal(barrier, inc=1, device_id=me.partner, device_id_type=MESH)
     return barrier
 
@@ -93,21 +102,12 @@
     landing = pl.multiple_of(at * CELL, CELL)
     mine = me.own // 16
 
-    def one(q, carry):
-        peer = me.peer(first, count, q)
-        rows = pl.ds(pl.multiple_of(peer * CELL, CELL), CELL)
-        itself = me.has_self & (peer == me.own)
-
-        @pl.when(itself)
-        def _():
-            pltpu.make_async_copy(
-                src.at[rows], dst.at[pl.ds(landing, CELL)], recv_sem.at[mine]
-            ).start()
-
-        @pl.when(jnp.logical_not(itself))
+    for peer in me.peers(first, count):
+
+        @pl.when(jnp.logical_not(me.has_self & (peer == me.own)))
         def _():
             pltpu.make_async_remote_copy(
-                src_ref=src.at[rows],
+                src_ref=src.at[pl.ds(pl.multiple_of(peer * CELL, CELL), CELL)],
                 dst_ref=dst.at[pl.ds(landing, CELL)],
                 send_sem=send_sem,
                 recv_sem=recv_sem.at[mine],
@@ -115,9 +115,13 @@
                 device_id_type=MESH,
             ).start()
 
-        return carry
-
-    lax.fori_loop(0, count, one, 0)
+    @pl.when(me.has_self & (me.own >= first) & (me.own < first + count))
+    def _():
+        pltpu.make_async_copy(
+            src.at[pl.ds(pl.multiple_of(me.own * CELL, CELL), CELL)],
+            dst.at[pl.ds(landing, CELL)],
+            recv_sem.at[mine],
+        ).start()
 
 
 def await_sends(me, src, dst, send_sem, recv_sem):
@@ -196,10 +200,9 @@
     back, placed, send, arrived, wq, wo, f1, f2, kk, marks, vt, qt, ctxv, s0, s1, p0, p1, m0, m1, table,
     send_sem, recv_sem, wloc_sem, wsend_sem, wrecv_sem, ksend_sem, krecv_sem,
     vsend_sem, vrecv_sem, bsend_sem, brecv_sem, rsend_sem, rrecv_sem,
-    out_sem, load_sem,
+    out_sem, load_sem, psend_sem, precv_sem,
 ):
     me = Place()
-    barrier = greet(me)
     loads = [
         pltpu.make_async_copy(src, dst, load_sem.at[i])
         for i, (src, dst) in enumerate(
@@ -214,6 +217,7 @@
     ]
     for copy in loads:
         copy.start()
+    barrier = greet(me)
     loads[0].wait()
     slots = local_slots(rank[...], me.s)
     s_refs, p_refs, m_refs = (s0, s1), (p0, p1), (m0, m1)
@@ -495,35 +499,49 @@
         start = pl.multiple_of(half * HALF + group * GROUP, GROUP)
         return relay(me, back, start, GROUP, rsend_sem.at[group], recv.at[group])
 
-    def hand_on(groups):
+    def hand_on(groups, awaited):
         for group in groups:
             passing(me.c, group, brecv_sem).wait_recv()
             passing(me.c, group, rrecv_sem).start()
-        for group in groups:
+        for group in awaited:
             passing(1 - me.c, group, rrecv_sem).wait_recv()
 
-    hand_on([me.group(0), me.group(2)])
-
     def place_early(i, carry):
-        rows = pl.ds(pl.multiple_of(i * 256, 256), 256)
-        column = slot_column(local_slots(rank[:, rows], me.s))
+        start = pl.multiple_of(me.c * HALF + i * 256, 256)
+        column = slot_column(local_slots(rank[:, pl.ds(start, 256)], me.s))
         total = None
         for base in group_bases(me.y):
             value = dot(picks(column, base), back[pl.ds(base, GROUP), :])
             total = value if total is None else total + value
-        placed[rows, :] = total.astype(BF16)
+        placed[pl.ds(start, 256), :] = total.astype(BF16)
         return carry
 
-    lax.fori_loop(0, LENGTH // 256, place_early, 0)
-    outs = [pltpu.make_async_copy(placed, part_ref, out_sem.at[4])]
-    outs[0].start()
-    hand_on([me.group(3), me.group(1)])
+    def placed_half(half):
+        start = pl.multiple_of(half * HALF, HALF)
+        rows = pl.ds(start, HALF)
+        return (
+            relay(me, placed, start, HALF, psend_sem, precv_sem),
+            pltpu.make_async_copy(placed.at[rows], part_ref.at[rows], out_sem.at[4 + half]),
+        )
+
+    hand_on([me.group(0), me.group(2)], [me.group(0), me.group(2)])
+    lax.fori_loop(0, HALF // 256, place_early, 0)
+    to_partner, own_out = placed_half(me.c)
+    from_partner, partner_out = placed_half(1 - me.c)
+    to_partner.start()
+    own_out.start()
+    hand_on([me.group(3)], [])
+    from_partner.wait_recv()
+    partner_out.start()
+    hand_on([me.group(1)], [me.group(3), me.group(1)])
+    outs = [own_out, partner_out]
     for i, base in enumerate(group_bases(1 - me.y)):
         copy = pltpu.make_async_copy(
             back.at[pl.ds(base, GROUP)], late_ref.at[pl.ds(i * GROUP, GROUP)], out_sem.at[i]
         )
         copy.start()
         outs.append(copy)
+    to_partner.wait_send()
     for group in range(GROUPS):
         passing(me.c, group, rrecv_sem).wait_send()
     for copy in outs:
@@ -586,7 +604,7 @@
             VMEM((8, 256), F32),
             pltpu.SMEM((4, 16), jnp.int32),
             dma, dma((4,)), dma((4,)), dma((4,)), dma((4,)), dma((4,)), dma((4,)),
-            dma((4,)), dma((4,)), dma, dma((4,)), dma((4,)), dma((4,)), dma((5,)), dma((5,)),
+            dma((4,)), dma((4,)), dma, dma((4,)), dma((4,)), dma((4,)), dma((6,)), dma((5,)), dma, dma,
         ],
         compiler_params=pltpu.CompilerParams(collective_id=0, has_side_effects=True),
     )(

time: 90.4 us -> 89.1 us (0.986)
  no operation moved by 1% of the time
where the time goes in v5:
time: 89.1 us; the launch traced here: 88.9 us
  Pallas kernels  88.9 us (100%)
    pallas_call x1, Pallas kernels, body(): pl.pallas_call(layer_kernel, name='layer', out_shape=(shape((LENGTH, FEAT...  83.7 us
    pallas_call x1, Pallas kernels, body(): pl.pallas_call(place_kernel, name='place_rows', grid=(LENGTH // 1024,), o...  5.18 us

profile of v5, /device:TPU:97, one launch (start us, length us, event | category | flops | bytes accessed | tf_op | source)
XLA Modules:
  0.0 88.9 jit_solution(2675002992510184133)
XLA Ops:
  0.0 83.7 %layer.1 = (bf16[2048,512]{1,0:T(8,128)(2,1)}, bf16[1024,512]{1,0:T(8,128)(2,1)}) custom-call(bf16[2048,512]{1,0:T(8,128)(2,1)} %points_in.1, s32[1,2048]{1,0:T(1,128)} %bitcast.3, s32[1,4]{1,0:T(1,128)} %counts_in.1, f32[1,512]{1,0:T(1,128)} %bitcast.5, bf16[3,512,256]{2,1,0:T(8,128)(2,1)} %w_qkv.1, bf16[256,512]{1,0:T(8,128)(2,1)} %w_out.1, ...), custom_call_target="tpu_custom_call" | custom-call | tf_op jit(solution)/shard_map/layer/pallas_call | solution.py:574
  83.7 5.2 %place_rows.1 = bf16[2048,512]{1,0:T(8,128)(2,1)} custom-call(s32[1,2048]{1,0:T(1,128)} %bitcast.4, bf16[2048,512]{1,0:T(8,128)(2,1)} %get-tuple-element.7.part, bf16[1024,512]{1,0:T(8,128)(2,1)} %get-tuple-element.8.late), custom_call_target="tpu_custom_call" | custom-call | tf_op jit(solution)/shard_map/place_rows/pallas_call | solution.py:615

commit v6 on v5

--- a/solution.py
+++ b/solution.py
@@ -38,6 +38,12 @@
     centred = values - average
     second = jnp.mean(centred * centred, axis=-1, keepdims=True)
     return (centred * lax.rsqrt(second + EPS) * gain).astype(BF16)
+
+
+def twice_gelu(x):
+    scale = math.sqrt(2.0 / math.pi)
+    inner = x * (scale + (scale * 0.044715) * (x * x))
+    return (x * (1.0 + jnp.tanh(inner))).astype(BF16)
 
 
 class Place:
@@ -445,10 +451,15 @@
     def block_context(n):
         begin, first = table[2, n] + 1, table[3, n]
         row = me.c * HALF + me.block(n) * 128
-        nth = patch_of(row + lax.broadcasted_iota(jnp.int32, (128, FEAT), 0)) - first
+        place = lax.broadcasted_iota(jnp.int32, (128, FEAT), 0)
         value = ctxv[begin]
         for e in range(1, 4):
-            value = jnp.where(nth >= e, ctxv[jnp.minimum(begin + e, ITEMS)], value)
+            patch = first + e
+            start = jnp.where(
+                patch == 1, c1, jnp.where(patch == 2, c2, jnp.where(patch == 3, c3, LENGTH))
+            )
+            other = ctxv[jnp.minimum(begin + e, ITEMS)]
+            value = jnp.where(place >= start - row, other, value)
         return value
 
     def finish(n, blocks):
@@ -460,11 +471,11 @@
         middle = (arrived[rows, :].astype(F32) + attn.astype(BF16).astype(F32)).astype(BF16)
         middle = middle.astype(F32)
         normed = norm_rows(middle, gain_mlp[...])
-        result = middle
+        total = None
         for half in range(2):
-            hidden = jax.nn.gelu(dot(normed, f1[half]), approximate=True).astype(BF16)
-            result = result + dot(hidden, f2[half])
-        send[rows, :] = result.astype(BF16)
+            value = dot(twice_gelu(dot(normed, f1[half])), f2[half])
+            total = value if total is None else total + value
+        send[rows, :] = (middle + 0.5 * total).astype(BF16)
         send_cells(me, block * 8, blocks * 8, send, back, me.s, bsend_sem, brecv_sem)
 
     def stretch(k, carry):
@@ -530,17 +541,34 @@
     from_partner, partner_out = placed_half(1 - me.c)
     to_partner.start()
     own_out.start()
-    hand_on([me.group(3)], [])
-    from_partner.wait_recv()
-    partner_out.start()
-    hand_on([me.group(1)], [me.group(3), me.group(1)])
+    def late_rows(half, j):
+        group = me.group(j)
+        src = back.at[pl.ds(pl.multiple_of(half * HALF + group * GROUP, GROUP), GROUP)]
+        spot = half * 2 + lax.rem(group, 2)
+        dst = late_ref.at[pl.ds(pl.multiple_of(spot * GROUP, GROUP), GROUP)]
+        there = pltpu.make_async_remote_copy(
+            src_ref=src,
+            dst_ref=dst,
+            send_sem=rsend_sem.at[group],
+            recv_sem=rrecv_sem.at[group],
+            device_id=me.partner,
+            device_id_type=MESH,
+        )
+        return src, dst, there
+
     outs = [own_out, partner_out]
-    for i, base in enumerate(group_bases(1 - me.y)):
-        copy = pltpu.make_async_copy(
-            back.at[pl.ds(base, GROUP)], late_ref.at[pl.ds(i * GROUP, GROUP)], out_sem.at[i]
-        )
-        copy.start()
-        outs.append(copy)
+    for j in (3, 1):
+        passing(me.c, me.group(j), brecv_sem).wait_recv()
+        src, dst, there = late_rows(me.c, j)
+        there.start()
+        here = pltpu.make_async_copy(src, dst, out_sem.at[j // 2])
+        here.start()
+        outs.append(here)
+        if j == 3:
+            from_partner.wait_recv()
+            partner_out.start()
+    for j in (3, 1):
+        late_rows(1 - me.c, j)[2].wait_recv()
     to_partner.wait_send()
     for group in range(GROUPS):
         passing(me.c, group, rrecv_sem).wait_send()

time: 89.1 us -> 88.2 us (0.990)
  no operation moved by 1% of the time
where the time goes in v6:
time: 88.2 us; the launch traced here: 88.1 us
  Pallas kernels  88.1 us (100%)
    pallas_call x1, Pallas kernels, body(): pl.pallas_call(layer_kernel, name='layer', out_shape=(shape((LENGTH, FEAT...  82.9 us
    pallas_call x1, Pallas kernels, body(): pl.pallas_call(place_kernel, name='place_rows', grid=(LENGTH // 1024,), o...  5.18 us

profile of v6, /device:TPU:97, one launch (start us, length us, event | category | flops | bytes accessed | tf_op | source)
XLA Modules:
  0.0 88.1 jit_solution(11559744006381316911)
XLA Ops:
  0.0 82.9 %layer.1 = (bf16[2048,512]{1,0:T(8,128)(2,1)}, bf16[1024,512]{1,0:T(8,128)(2,1)}) custom-call(bf16[2048,512]{1,0:T(8,128)(2,1)} %points_in.1, s32[1,2048]{1,0:T(1,128)} %bitcast.3, s32[1,4]{1,0:T(1,128)} %counts_in.1, f32[1,512]{1,0:T(1,128)} %bitcast.5, bf16[3,512,256]{2,1,0:T(8,128)(2,1)} %w_qkv.1, bf16[256,512]{1,0:T(8,128)(2,1)} %w_out.1, ...), custom_call_target="tpu_custom_call" | custom-call | tf_op jit(solution)/shard_map/layer/pallas_call | solution.py:602
  82.9 5.2 %place_rows.1 = bf16[2048,512]{1,0:T(8,128)(2,1)} custom-call(s32[1,2048]{1,0:T(1,128)} %bitcast.4, bf16[2048,512]{1,0:T(8,128)(2,1)} %get-tuple-element.7.part, bf16[1024,512]{1,0:T(8,128)(2,1)} %get-tuple-element.8.late), custom_call_target="tpu_custom_call" | custom-call | tf_op jit(solution)/shard_map/place_rows/pallas_call | solution.py:643

commit v7 on v6

--- a/solution.py
+++ b/solution.py
@@ -332,16 +332,22 @@
         place = me.c * 8 + group * 2
         normed = norm_rows(arrived[rows, :].astype(F32), gain_attn[...])
         row = lax.broadcasted_iota(jnp.int32, (128, 128), 0)
+        to_keys, to_values = exchange(me.c, group)
         for half in range(2):
-            keys = dot(normed, wq[half, 1]).astype(BF16)
             values = dot(normed, wq[half, 2])
             for p in range(2):
                 pair, cols = 2 * half + p, slice(p * 128, (p + 1) * 128)
                 for b in range(2):
-                    kk[pair, place + b] = keys[b * 128 : (b + 1) * 128, cols]
                     vt[pair, place + b, 0:128, :] = values[b * 128 : (b + 1) * 128, cols].T.astype(
                         BF16
                     )
+        for half in range(2):
+            keys = dot(normed, wq[half, 1]).astype(BF16)
+            for p in range(2):
+                pair, cols = 2 * half + p, slice(p * 128, (p + 1) * 128)
+                for b in range(2):
+                    kk[pair, place + b] = keys[b * 128 : (b + 1) * 128, cols]
+        to_values.start()
         for half in range(2):
             queries = dot(normed, wq[half, 0]) * QSCALE
             for p in range(2):
@@ -353,6 +359,8 @@
                     qt[block, pair, 0:128, 128:256] = jnp.where(row >= HDIM, turned, 0.0).astype(
                         BF16
                     )
+            if half == 0:
+                to_keys.start()
 
     def exchange(half, group):
         place = half * 8 + group * 2
@@ -380,8 +388,6 @@
             rsend_sem.at[group], recv_sem.at[group],
         ).wait_recv()
         project(group)
-        for copy in exchange(me.c, group):
-            copy.start()
     for j in range(GROUPS):
         for copy in exchange(1 - me.c, me.group(j)):
             copy.wait_recv()
@@ -419,7 +425,7 @@
         )
         ctxv[item, :, pair * 128 : (pair + 1) * 128] = result.T.astype(BF16)
 
-    def step(item, pair):
+    def step(item, pair, settled=False):
         now, other = pair % 2, 1 - pair % 2
         after, after_pair = (item, pair + 1) if pair < 3 else (item + 1, 0)
         before, before_pair = (item, pair - 1) if pair > 0 else (item - 1, 3)
@@ -429,10 +435,11 @@
             if part % 3 == 0:
                 high = score(after_pair, after, part // 3, other, high)
             raise_part(now, part, top)
-            if part % 2 == 1:
+            if part % 2 == 1 and not settled:
                 total = weigh(before_pair, before, other, (part - 1) * 128, 256, total)
-        total = weigh(before_pair, before, other, 1024, 128, total)
-        conclude(before_pair, before, total)
+        if not settled:
+            total = weigh(before_pair, before, other, 1024, 128, total)
+            conclude(before_pair, before, total)
         settle(other, high)
 
     def one_item(item, carry):
@@ -440,9 +447,6 @@
             step(item, pair)
         return carry
 
-    table[0, 0] = table[0, 1]
-    table[1, 0] = table[1, 1]
-    p1[...] = jnp.zeros_like(p1)
     high = None
     for part in range(3):
         high = score(0, 1, part, 0, high)
@@ -481,7 +485,9 @@
     def stretch(k, carry):
         low = jnp.where(k == 0, 1, jnp.where(k == 1, 5, 2 * k + 2))
         high = jnp.where(k == 0, 5, 2 * k + 4)
-        lax.fori_loop(low, high, one_item, 0)
+        for pair in range(4):
+            step(low, pair, settled=pair == 0)
+        lax.fori_loop(low + 1, high, one_item, 0)
         total = None
         for part in range(4):
             total = weigh(3, high - 1, 1, part * 256, 256, total)

time: 88.2 us -> 88.8 us (level)
  no operation moved by 1% of the time
where the time goes in v7:
time: 88.8 us; the launch traced here: 88.7 us
  Pallas kernels  88.7 us (100%)
    pallas_call x1, Pallas kernels, body(): pl.pallas_call(layer_kernel, name='layer', out_shape=(shape((LENGTH, FEAT...  83.5 us
    pallas_call x1, Pallas kernels, body(): pl.pallas_call(place_kernel, name='place_rows', grid=(LENGTH // 1024,), o...  5.18 us

profile of v7, /device:TPU:97, one launch (start us, length us, event | category | flops | bytes accessed | tf_op | source)
XLA Modules:
  0.0 88.7 jit_solution(14987780007709095993)
XLA Ops:
  0.0 83.5 %layer.1 = (bf16[2048,512]{1,0:T(8,128)(2,1)}, bf16[1024,512]{1,0:T(8,128)(2,1)}) custom-call(bf16[2048,512]{1,0:T(8,128)(2,1)} %points_in.1, s32[1,2048]{1,0:T(1,128)} %bitcast.3, s32[1,4]{1,0:T(1,128)} %counts_in.1, f32[1,512]{1,0:T(1,128)} %bitcast.5, bf16[3,512,256]{2,1,0:T(8,128)(2,1)} %w_qkv.1, bf16[256,512]{1,0:T(8,128)(2,1)} %w_out.1, ...), custom_call_target="tpu_custom_call" | custom-call | tf_op jit(solution)/shard_map/layer/pallas_call | solution.py:608
  83.5 5.2 %place_rows.1 = bf16[2048,512]{1,0:T(8,128)(2,1)} custom-call(s32[1,2048]{1,0:T(1,128)} %bitcast.4, bf16[2048,512]{1,0:T(8,128)(2,1)} %get-tuple-element.7.part, bf16[1024,512]{1,0:T(8,128)(2,1)} %get-tuple-element.8.late), custom_call_target="tpu_custom_call" | custom-call | tf_op jit(solution)/shard_map/place_rows/pallas_call | solution.py:649

commit v8 on v6

--- a/solution.py
+++ b/solution.py
@@ -332,16 +332,22 @@
         place = me.c * 8 + group * 2
         normed = norm_rows(arrived[rows, :].astype(F32), gain_attn[...])
         row = lax.broadcasted_iota(jnp.int32, (128, 128), 0)
+        to_keys, to_values = exchange(me.c, group)
         for half in range(2):
-            keys = dot(normed, wq[half, 1]).astype(BF16)
             values = dot(normed, wq[half, 2])
             for p in range(2):
                 pair, cols = 2 * half + p, slice(p * 128, (p + 1) * 128)
                 for b in range(2):
-                    kk[pair, place + b] = keys[b * 128 : (b + 1) * 128, cols]
                     vt[pair, place + b, 0:128, :] = values[b * 128 : (b + 1) * 128, cols].T.astype(
                         BF16
                     )
+        for half in range(2):
+            keys = dot(normed, wq[half, 1]).astype(BF16)
+            for p in range(2):
+                pair, cols = 2 * half + p, slice(p * 128, (p + 1) * 128)
+                for b in range(2):
+                    kk[pair, place + b] = keys[b * 128 : (b + 1) * 128, cols]
+        to_values.start()
         for half in range(2):
             queries = dot(normed, wq[half, 0]) * QSCALE
             for p in range(2):
@@ -353,6 +359,8 @@
                     qt[block, pair, 0:128, 128:256] = jnp.where(row >= HDIM, turned, 0.0).astype(
                         BF16
                     )
+            if half == 0:
+                to_keys.start()
 
     def exchange(half, group):
         place = half * 8 + group * 2
@@ -380,8 +388,6 @@
             rsend_sem.at[group], recv_sem.at[group],
         ).wait_recv()
         project(group)
-        for copy in exchange(me.c, group):
-            copy.start()
     for j in range(GROUPS):
         for copy in exchange(1 - me.c, me.group(j)):
             copy.wait_recv()

time: 88.2 us -> 88.6 us (level)
  no operation moved by 1% of the time
where the time goes in v8:
time: 88.6 us; the launch traced here: 88.5 us
  Pallas kernels  88.4 us (100%)
    pallas_call x1, Pallas kernels, body(): pl.pallas_call(layer_kernel, name='layer', out_shape=(shape((LENGTH, FEAT...  83.3 us
    pallas_call x1, Pallas kernels, body(): pl.pallas_call(place_kernel, name='place_rows', grid=(LENGTH // 1024,), o...  5.18 us

profile of v8, /device:TPU:97, one launch (start us, length us, event | category | flops | bytes accessed | tf_op | source)
XLA Modules:
  0.0 88.5 jit_solution(10576144158359386889)
XLA Ops:
  0.0 83.3 %layer.1 = (bf16[2048,512]{1,0:T(8,128)(2,1)}, bf16[1024,512]{1,0:T(8,128)(2,1)}) custom-call(bf16[2048,512]{1,0:T(8,128)(2,1)} %points_in.1, s32[1,2048]{1,0:T(1,128)} %bitcast.3, s32[1,4]{1,0:T(1,128)} %counts_in.1, f32[1,512]{1,0:T(1,128)} %bitcast.5, bf16[3,512,256]{2,1,0:T(8,128)(2,1)} %w_qkv.1, bf16[256,512]{1,0:T(8,128)(2,1)} %w_out.1, ...), custom_call_target="tpu_custom_call" | custom-call | tf_op jit(solution)/shard_map/layer/pallas_call | solution.py:608
  83.3 5.2 %place_rows.1 = bf16[2048,512]{1,0:T(8,128)(2,1)} custom-call(s32[1,2048]{1,0:T(1,128)} %bitcast.4, bf16[2048,512]{1,0:T(8,128)(2,1)} %get-tuple-element.7.part, bf16[1024,512]{1,0:T(8,128)(2,1)} %get-tuple-element.8.late), custom_call_target="tpu_custom_call" | custom-call | tf_op jit(solution)/shard_map/place_rows/pallas_call | solution.py:649
